TPU v7x, 128 devices: a whole 4x4x4 slice. The times are simulated.
128 devices in a mesh: dp: 16 (over x, z), tensor: 8 (over y, core).
Axes of the slice: x: 4, y: 4, z: 4, core: 2. Of those that a mesh axis runs over, the one named last changes fastest.
Arguments:
- activations: bfloat16 [256, 256, 14336], P('dp', None, 'tensor'), may hold values from -6 to 6
- out_grads: bfloat16 [256, 256, 4096], P('dp', None, 'tensor'), may hold values from -0.29882812 to 0.29882812
- lengths: int32 [256], P('dp'), may hold values from 1 to 256, 49152 in all
- bank_in: bfloat16 [16, 128, 64], replicated, may hold values from -0.046875 to 0.046875
- index_in: int32 [112], P('tensor'), may hold values from 0 to 15
- bank_out: bfloat16 [16, 128, 64], replicated, may hold values from -0.09375 to 0.09375
- index_out: int32 [32], P('tensor'), may hold values from 0 to 15
- prior_cov: float32 [4096, 4096], P('dp'), may hold values from -1 to 5, as said below
- val_grads: float32 [4096, 512], P('dp', 'tensor'), may hold values from -0.3 to 0.3
Outputs:
- scores: float32 [256, 512], P('dp', 'tensor')
Inputs may be any that keep to these rules, and one draw needn't show every extreme that they name: `lengths`: the longest rollout uses all 256 slots. `prior_cov`: symmetric and positive definite.
All inputs are finite; a program needn't handle non-finite values. No bound on the sum of `lengths` on one device may be relied on, other than what follows from the above.
Results may differ from a plain program's by a relative error of at most 0.0003.
Values sent between devices are 32-bit elements; how exact they have to be, the bound alone decides.
No kernel may reach another device: no remote copies, remote signals or barrier semaphores. Data moves between devices by JAX's collectives and lax.ppermute only.
A program may use at most 128 MiB of HBM per device.

v0:
```python
import jax
import jax.numpy as jnp
from jax import lax
from jax.sharding import PartitionSpec as P

ITERS = 6


HIGH = lax.Precision.HIGHEST


def local_projection(bank, index_table):
    bank_count = bank.shape[0]
    onehot = (index_table[:, None] == jnp.arange(bank_count, dtype=jnp.int32)[None, :]).astype(
        jnp.bfloat16
    )
    flat = jnp.dot(
        onehot,
        bank.reshape(bank_count, bank.shape[1] * bank.shape[2]),
        preferred_element_type=jnp.float32,
    )
    return flat.astype(jnp.bfloat16).reshape(index_table.shape[0] * bank.shape[1], bank.shape[2])


def rollout_factors(summed, lengths_here):
    low_rank = summed.shape[2] // 2
    slot_count = summed.shape[1]
    used = (jnp.arange(slot_count, dtype=jnp.int32)[None, :] < lengths_here[:, None]).astype(
        jnp.float32
    )
    grad_low = summed[:, :, :low_rank] * used[:, :, None]
    act_low = summed[:, :, low_rank:]
    products = jnp.einsum("rsk,rsl->rkl", grad_low, act_low, precision=HIGH)
    return products.reshape(summed.shape[0], low_rank * low_rank)


def per_device(
    activations, out_grads, lengths, bank_in, index_in, bank_out, index_out, prior_cov, val_grads
):
    proj_in = local_projection(bank_in, index_in)
    proj_out = local_projection(bank_out, index_out)
    roll_here = activations.shape[0]
    grad_low = jnp.einsum("rsd,dk->rsk", out_grads, proj_out, preferred_element_type=jnp.float32)
    act_low = jnp.einsum("rsf,fk->rsk", activations, proj_in, preferred_element_type=jnp.float32)
    summed = lax.psum(jnp.concatenate((grad_low, act_low), axis=2), "tensor")
    all_factors = lax.all_gather(rollout_factors(summed, lengths), "dp", axis=0, tiled=True)
    cov_here = prior_cov.shape[0]
    feature_count = prior_cov.shape[1]
    first_row = lax.axis_index("dp") * cov_here
    rollouts_total = all_factors.shape[0]
    own_columns = lax.dynamic_slice_in_dim(all_factors, first_row, cov_here, 1)
    outer_sum = lax.dot_general(own_columns, all_factors, (((0,), (0,)), ((), ())), precision=HIGH)
    covariance = prior_cov + outer_sum / rollouts_total
    diag_part = jnp.trace(lax.dynamic_slice_in_dim(covariance, first_row, cov_here, 1))
    residual = val_grads
    solution = jnp.zeros_like(val_grads)
    trace_total, norm_now = lax.psum((diag_part, jnp.sum(residual * residual, axis=0)), "dp")
    damping = 0.1 * trace_total / feature_count
    direction = residual
    for iteration in range(ITERS):
        contract_block_rows = lax.all_gather(direction, "dp", axis=0, tiled=True)
        contract_columns = lax.slice_in_dim(covariance, 0, contract_block_rows.shape[0], axis=1)
        image = (
            jnp.zeros_like(direction)
            + jnp.dot(contract_columns, contract_block_rows, precision=HIGH)
            + damping * direction
        )
        curvature = lax.psum(jnp.sum(direction * image, axis=0), "dp")
        alpha = norm_now / curvature
        solution = solution + alpha * direction
        residual = residual - alpha * image
        if iteration + 1 < ITERS:
            norm_next = lax.psum(jnp.sum(residual * residual, axis=0), "dp")
            direction = residual + norm_next / norm_now * direction
            norm_now = norm_next
    own_factors = lax.dynamic_slice_in_dim(
        all_factors, lax.axis_index("dp") * roll_here, roll_here, 0
    )
    empty = jnp.zeros((roll_here, solution.shape[1]), jnp.float32)
    block_rows = lax.all_gather(solution, "dp", axis=0, tiled=True)
    columns = lax.slice_in_dim(own_factors, 0, block_rows.shape[0], axis=1)
    return empty + jnp.dot(columns, block_rows, precision=HIGH)


def solution(mesh):
    return jax.shard_map(
        per_device,
        mesh=mesh,
        in_specs=(
            P("dp", None, "tensor"),
            P("dp", None, "tensor"),
            P("dp"),
            P(),
            P("tensor"),
            P(),
            P("tensor"),
            P("dp", None),
            P("dp", "tensor"),
        ),
        out_specs=P("dp", "tensor"),
        check_vma=False,
    )
```

profile of v0, /device:TPU:0, one launch (start us, length us, event | category | flops | bytes accessed | tf_op | source)
XLA Modules:
  0.0 902.9 jit_solution(5091932144817809208)
XLA Ops:
  11.8 9.9 %convolution_bitcast_fusion.1 = f32[16,256,64]{1,2,0:T(8,128)S(1)} fusion(bf16[16,256,1792]{2,1,0:T(8,128)(2,1)} %param.9, bf16[1792,64]{1,0:T(8,128)(2,1)S(1)} %reshape.53), kind=kOutput, calls=%fused_computation.6 | convolution fusion | flops 939524096 | bytes 15958016 | tf_op jit(solution)/shard_map/rsf,fk->rsk/dot_general | solution.py:44
  23.1 1.4 pad_maximum_fusion
  24.7 68.2 %all-reduce.3.cloned.1.call-done = f32[16,256,128]{1,2,0:T(8,128)} async-done(((f32[16,256,128]{1,2,0:T(8,128)}), f32[16,256,128]{1,2,0:T(8,128)}) %all-reduce.3.cloned.1.call-update) | async-done | bytes 2097168 | tf_op jit(solution)/shard_map/psum | solution.py:45
  92.9 2.7 fusion.3
  97.2 50.6 %all-gather.9.cloned.1.call-done = f32[256,4096]{1,0:T(8,128)} async-done(((f32[16,4096]{1,0:T(8,128)}), f32[256,4096]{1,0:T(8,128)}) %all-gather.9.cloned.1.call-update) | async-done | bytes 4194320 | tf_op jit(solution)/shard_map/all_gather | solution.py:46
  147.8 7.5 fusion
  155.3 2.0 copy-done
  157.9 39.4 %psum.100 = f32[]{:T(128)} all-reduce(f32[]{:T(128)} %select_reduce_fusion), channel_id=1, replica_groups=mesh['dp'=16,'tensor'=8] {'dp'}, use_global_device_ids=true, to_apply=%region_4.5 | all-reduce | flops 1 | bytes 8 | tf_op jit(solution)/shard_map/psum | solution.py:57
  198.0 6.5 multiply_reduce_fusion.9
  204.5 35.5 %all-reduce = (f32[64]{0:T(128)S(1)}, f32[64]{0:T(128)S(1)}) all-reduce(f32[64]{0:T(128)S(1)} %get-tuple-element.6, f32[64]{0:T(128)S(1)} %get-tuple-element.5), channel_id=1, replica_groups=mesh['dp'=16,'tensor'=8] {'dp'}, use_global_device_ids=true, to_apply=%region_2.3 | all-reduce | flops 128 | bytes 1024 | tf_op jit(solution)/shard_map/psum | solution.py:57
  240.2 37.5 %psum.102 = f32[64]{0:T(128)S(1)} all-reduce(f32[64]{0:T(128)S(1)} %multiply_reduce_fusion.8), channel_id=1, replica_groups=mesh['dp'=16,'tensor'=8] {'dp'}, use_global_device_ids=true, to_apply=%region_8.9 | all-reduce | flops 64 | bytes 512 | tf_op jit(solution)/shard_map/psum | solution.py:73
  278.4 39.8 %all-gather.13.cloned.1.call-done = f32[4096,64]{0,1:T(8,128)} async-done(((f32[256,64]{0,1:T(8,128)}), f32[4096,64]{0,1:T(8,128)}) %all-gather.13.cloned.1.call-update) | async-done | bytes 1048592 | tf_op jit(solution)/shard_map/all_gather | solution.py:61
  318.3 6.5 multiply_reduce_fusion.7
  324.8 38.2 %psum.103 = f32[64]{0:T(128)S(1)} all-reduce(f32[64]{0:T(128)S(1)} %get-tuple-element.16), channel_id=1, replica_groups=mesh['dp'=16,'tensor'=8] {'dp'}, use_global_device_ids=true, to_apply=%region_10.11 | all-reduce | flops 64 | bytes 512 | tf_op jit(solution)/shard_map/psum | solution.py:68
  363.2 35.5 %psum.104 = f32[64]{0:T(128)S(1)} all-reduce(f32[64]{0:T(128)S(1)} %get-tuple-element.13), channel_id=1, replica_groups=mesh['dp'=16,'tensor'=8] {'dp'}, use_global_device_ids=true, to_apply=%region_12.13 | all-reduce | flops 64 | bytes 512 | tf_op jit(solution)/shard_map/psum | solution.py:73
  399.5 41.3 %all-gather.15.cloned.1.call-done = f32[4096,64]{0,1:T(8,128)} async-done(((f32[256,64]{0,1:T(8,128)}), f32[4096,64]{0,1:T(8,128)}) %all-gather.15.cloned.1.call-update) | async-done | bytes 1048592 | tf_op jit(solution)/shard_map/all_gather | solution.py:61
  440.7 6.5 multiply_reduce_fusion.5
  447.3 38.2 %psum.105 = f32[64]{0:T(128)S(1)} all-reduce(f32[64]{0:T(128)S(1)} %get-tuple-element.18), channel_id=1, replica_groups=mesh['dp'=16,'tensor'=8] {'dp'}, use_global_device_ids=true, to_apply=%region_14.15 | all-reduce | flops 64 | bytes 512 | tf_op jit(solution)/shard_map/psum | solution.py:68
  485.7 35.5 %psum.106 = f32[64]{0:T(128)S(1)} all-reduce(f32[64]{0:T(128)S(1)} %get-tuple-element.11), channel_id=1, replica_groups=mesh['dp'=16,'tensor'=8] {'dp'}, use_global_device_ids=true, to_apply=%region_16.17 | all-reduce | flops 64 | bytes 512 | tf_op jit(solution)/shard_map/psum | solution.py:73
  522.1 41.1 %all-gather.17.cloned.1.call-done = f32[4096,64]{0,1:T(8,128)} async-done(((f32[256,64]{0,1:T(8,128)}), f32[4096,64]{0,1:T(8,128)}) %all-gather.17.cloned.1.call-update) | async-done | bytes 1048592 | tf_op jit(solution)/shard_map/all_gather | solution.py:61
  563.2 6.5 multiply_reduce_fusion.3
  569.7 38.2 %psum.107 = f32[64]{0:T(128)S(1)} all-reduce(f32[64]{0:T(128)S(1)} %get-tuple-element.20), channel_id=1, replica_groups=mesh['dp'=16,'tensor'=8] {'dp'}, use_global_device_ids=true, to_apply=%region_18.19 | all-reduce | flops 64 | bytes 512 | tf_op jit(solution)/shard_map/psum | solution.py:68
  608.1 35.5 %psum.108 = f32[64]{0:T(128)S(1)} all-reduce(f32[64]{0:T(128)S(1)} %get-tuple-element.9), channel_id=1, replica_groups=mesh['dp'=16,'tensor'=8] {'dp'}, use_global_device_ids=true, to_apply=%region_20.21 | all-reduce | flops 64 | bytes 512 | tf_op jit(solution)/shard_map/psum | solution.py:73
  644.4 41.3 %all-gather.19.cloned.1.call-done = f32[4096,64]{0,1:T(8,128)} async-done(((f32[256,64]{0,1:T(8,128)}), f32[4096,64]{0,1:T(8,128)}) %all-gather.19.cloned.1.call-update) | async-done | bytes 1048592 | tf_op jit(solution)/shard_map/all_gather | solution.py:61
  685.6 6.5 multiply_reduce_fusion.1
  692.2 38.2 %psum.109 = f32[64]{0:T(128)S(1)} all-reduce(f32[64]{0:T(128)S(1)} %get-tuple-element.22), channel_id=1, replica_groups=mesh['dp'=16,'tensor'=8] {'dp'}, use_global_device_ids=true, to_apply=%region_22.23 | all-reduce | flops 64 | bytes 512 | tf_op jit(solution)/shard_map/psum | solution.py:68
  730.6 35.5 %psum.110 = f32[64]{0:T(128)S(1)} all-reduce(f32[64]{0:T(128)S(1)} %multiply_reduce_fusion), channel_id=1, replica_groups=mesh['dp'=16,'tensor'=8] {'dp'}, use_global_device_ids=true, to_apply=%region_24.25 | all-reduce | flops 64 | bytes 512 | tf_op jit(solution)/shard_map/psum | solution.py:73
  766.8 41.3 %all-gather.21.cloned.1.call-done = f32[4096,64]{0,1:T(8,128)} async-done(((f32[256,64]{0,1:T(8,128)}), f32[4096,64]{0,1:T(8,128)}) %all-gather.21.cloned.1.call-update) | async-done | bytes 1048592 | tf_op jit(solution)/shard_map/all_gather | solution.py:61
  808.1 6.5 fusion.2
  814.7 38.2 %psum.111 = f32[64]{0:T(128)S(1)} all-reduce(f32[64]{0:T(128)S(1)} %fusion.2), channel_id=1, replica_groups=mesh['dp'=16,'tensor'=8] {'dp'}, use_global_device_ids=true, to_apply=%region_26.27 | all-reduce | flops 64 | bytes 512 | tf_op jit(solution)/shard_map/psum | solution.py:68
  853.6 39.9 %all-gather.23.cloned.1.call-done = f32[4096,64]{0,1:T(8,128)} async-done(((f32[256,64]{0,1:T(8,128)}), f32[4096,64]{0,1:T(8,128)}) %all-gather.23.cloned.1.call-update) | async-done | bytes 1048592 | tf_op jit(solution)/shard_map/all_gather | solution.py:80
  893.5 2.8 fusion.8
  (72 shorter events, 14.8 us)
Async XLA Ops:
  6.5 4.8 copy-start.8
  6.5 86.3 %all-reduce.3.cloned.1.call-start = ((), (), s32[]{:S(2)}) async-start(), calls=%async_computation | async-start | bytes 4194304 | tf_op jit(solution)/shard_map/psum | solution.py:45
  11.8 9.9 %copy-start.1 = (bf16[16,256,512]{2,1,0:T(8,128)(2,1)S(1)}, bf16[16,256,512]{2,1,0:T(8,128)(2,1)}, u32[]{:S(2)}) copy-start(bf16[16,256,512]{2,1,0:T(8,128)(2,1)} %param.10) | copy-start | bytes 12582916
  23.0 1.5 copy-start.9
  24.5 123.3 %all-gather.9.cloned.1.call-start = ((), (), s32[]{:S(2)}) async-start(), calls=%async_computation.1 | async-start | bytes 4456448 | tf_op jit(solution)/shard_map/all_gather | solution.py:46
  96.4 101.6 %all-gather.11.cloned.1.call-start = ((), (), s32[]{:S(2)}) async-start(), calls=%async_computation.2 | async-start | bytes 1114112 | tf_op jit(solution)/shard_map/all_gather | solution.py:61
  97.2 221.1 %all-gather.13.cloned.1.call-start = ((), (), s32[]{:S(2)}) async-start(), calls=%async_computation.3 | async-start | bytes 1114112 | tf_op jit(solution)/shard_map/all_gather | solution.py:61
  97.2 100.8 %copy-start.2 = (f32[256,64]{0,1:T(8,128)S(1)}, f32[256,64]{0,1:T(8,128)}, u32[]{:S(2)}) copy-start(f32[256,64]{0,1:T(8,128)} %param.17) | copy-start | bytes 196612
  155.3 2.0 copy-start
  278.4 120.3 %copy-start.3 = (f32[256,64]{0,1:T(8,128)S(1)}, f32[256,64]{0,1:T(8,128)}, u32[]{:S(2)}) copy-start(f32[256,64]{0,1:T(8,128)} %multiply_add_fusion.5) | copy-start | bytes 196612
  278.4 162.3 %all-gather.15.cloned.1.call-start = ((), (), s32[]{:S(2)}) async-start(), calls=%async_computation.4 | async-start | bytes 1114112 | tf_op jit(solution)/shard_map/all_gather | solution.py:61
  399.4 121.8 %copy-start.4 = (f32[256,64]{0,1:T(8,128)S(1)}, f32[256,64]{0,1:T(8,128)}, u32[]{:S(2)}) copy-start(f32[256,64]{0,1:T(8,128)} %multiply_add_fusion.4) | copy-start | bytes 196612
  399.4 163.8 %all-gather.17.cloned.1.call-start = ((), (), s32[]{:S(2)}) async-start(), calls=%async_computation.5 | async-start | bytes 1114112 | tf_op jit(solution)/shard_map/all_gather | solution.py:61
  521.8 121.8 %copy-start.5 = (f32[256,64]{0,1:T(8,128)S(1)}, f32[256,64]{0,1:T(8,128)}, u32[]{:S(2)}) copy-start(f32[256,64]{0,1:T(8,128)} %multiply_add_fusion.3) | copy-start | bytes 196612
  521.9 163.8 %all-gather.19.cloned.1.call-start = ((), (), s32[]{:S(2)}) async-start(), calls=%async_computation.6 | async-start | bytes 1114112 | tf_op jit(solution)/shard_map/all_gather | solution.py:61
  644.3 121.8 %copy-start.6 = (f32[256,64]{0,1:T(8,128)S(1)}, f32[256,64]{0,1:T(8,128)}, u32[]{:S(2)}) copy-start(f32[256,64]{0,1:T(8,128)} %multiply_add_fusion.2) | copy-start | bytes 196612
  644.3 163.8 %all-gather.21.cloned.1.call-start = ((), (), s32[]{:S(2)}) async-start(), calls=%async_computation.7 | async-start | bytes 1114112 | tf_op jit(solution)/shard_map/all_gather | solution.py:61
  766.8 86.1 %copy-start.7 = (f32[256,64]{0,1:T(8,128)S(1)}, f32[256,64]{0,1:T(8,128)}, u32[]{:S(2)}) copy-start(f32[256,64]{0,1:T(8,128)} %multiply_add_fusion.1) | copy-start | bytes 196612
  766.8 126.7 %all-gather.23.cloned.1.call-start = ((), (), s32[]{:S(2)}) async-start(), calls=%async_computation.8 | async-start | bytes 1114112 | tf_op jit(solution)/shard_map/all_gather | solution.py:80
Sparse Core Ops, SparseCore 0:
  24.6 68.1 all-reduce.2
  96.5 51.2 all-gather.8
  149.9 43.1 all-gather.10
  278.5 39.7 all-gather.12
  399.5 41.1 all-gather.14
  522.0 41.1 all-gather.16
  644.4 41.1 all-gather.18
  766.9 41.1 all-gather.20
  853.7 39.7 all-gather.22
where the time goes:
time: 903 us
  blocking collectives  445 us (49%)
  waiting for transfers between devices  364 us (40%)
  matrix products  64.7 us (7%)
  between operations  14.1 us (2%)
    all_gather x6, waiting for transfers between devices, per_device(): contract_block_rows = lax.all_gather(direction, 'dp', axis=0, tiled=True)  205 us
    psum x5, blocking collectives, per_device(): curvature = lax.psum(jnp.sum(direction * image, axis=0), 'dp')  191 us
    psum x5, blocking collectives, per_device(): norm_next = lax.psum(jnp.sum(residual * residual, axis=0), 'dp')  179 us
    psum x2, blocking collectives, per_device(): lax.psum((diag_part, jnp.sum(residual * residual, axis=0)), 'dp')  74.9 us
    psum x1, waiting for transfers between devices, per_device(): summed = lax.psum(jnp.concatenate((grad_low, act_low), axis=2), 'tensor')  68.2 us
    all_gather x1, waiting for transfers between devices, per_device(): lax.all_gather(rollout_factors(summed, lengths), 'dp', axis=0, tiled=True)  50.6 us
    all_gather x1, waiting for transfers between devices, per_device(): block_rows = lax.all_gather(solution, 'dp', axis=0, tiled=True)  39.9 us
    dot_general x6, matrix products, per_device(): jnp.dot(contract_columns, contract_block_rows, precision=HIGH)  39.3 us
  transfers between devices with their start and end apart: 9, of which 8 were waited for; matrix products, arithmetic and copies ran while one was open for 1% of the time, Pallas kernels for 0%

commit v1 on v0

v1 whole, which is shorter than its diff:
```python
import functools

import jax
import jax.numpy as jnp
from jax import lax
from jax.experimental import pallas as pl
from jax.experimental.pallas import tpu as pltpu
from jax.sharding import PartitionSpec as P

ITERS = 6
F32 = jnp.float32
BF16 = jnp.bfloat16
HIGHEST = lax.Precision.HIGHEST

NT = (((1,), (1,)), ((), ()))
NN = (((1,), (0,)), ((), ()))
TN = (((0,), (0,)), ((), ()))

SIDE = 4
CORES = 2
BLK = 256
VMEM = pl.BlockSpec(memory_space=pltpu.VMEM)
SMEM = pl.BlockSpec(memory_space=pltpu.SMEM)


def params(mib):
    return pltpu.CompilerParams(vmem_limit_bytes=mib << 20)


def split(value):
    high = value.astype(BF16)
    return high, (value - high.astype(F32)).astype(BF16)


def mm(a, b, dims):
    return lax.dot_general(a, b, dims, preferred_element_type=F32)


def mm3(a, b, dims):
    return mm(a[0], b[0], dims) + mm(a[1], b[0], dims) + mm(a[0], b[1], dims)


def along_z(step):
    return [(i, (i // SIDE) * SIDE + (i + step) % SIDE) for i in range(16)]


def along_x(step):
    return [(i, (i + step * SIDE) % 16) for i in range(16)]


def along_y(step):
    return [(i, (i + step * CORES) % 8) for i in range(8)]


def other_core():
    return [(i, i ^ 1) for i in range(8)]


def crossed(step, flip):
    pairs = []
    for dp in range(16):
        for tensor in range(8):
            table = along_x(step) if (tensor % CORES) ^ flip else along_z(step)
            pairs.append((dp * 8 + tensor, table[dp][1] * 8 + tensor))
    return pairs


def project_kernel(order, idx_in, idx_out, act, grad, bank_in, bank_out, out, proj_in, proj_out):
    @pl.when(pl.program_id(0) == 0)
    def _():
        for b in range(proj_in.shape[1] // 128):
            proj_in[:, b * 128 : (b + 1) * 128] = bank_in[idx_in[b]]
        for b in range(proj_out.shape[1] // 128):
            proj_out[:, b * 128 : (b + 1) * 128] = bank_out[idx_out[b]]

    out[0, :, 0:64] = mm(act[0], proj_in[...], NT)
    out[0, :, 64:128] = mm(grad[0], proj_out[...], NT)


def project(order, idx_in, idx_out, act, grad, bank_in_t, bank_out_t):
    count = order.shape[0]
    slots, width, model = act.shape[1], act.shape[2], grad.shape[2]
    return pl.pallas_call(
        project_kernel,
        out_shape=jax.ShapeDtypeStruct((count, slots, 128), F32),
        grid_spec=pltpu.PrefetchScalarGridSpec(
            num_scalar_prefetch=3,
            grid=(count,),
            in_specs=[
                pl.BlockSpec((1, slots, width), lambda i, o, a, b: (o[i], 0, 0)),
                pl.BlockSpec((1, slots, model), lambda i, o, a, b: (o[i], 0, 0)),
                pl.BlockSpec(bank_in_t.shape, lambda i, o, a, b: (0, 0, 0)),
                pl.BlockSpec(bank_out_t.shape, lambda i, o, a, b: (0, 0, 0)),
            ],
            out_specs=pl.BlockSpec((1, slots, 128), lambda i, o, a, b: (i, 0, 0)),
            scratch_shapes=[pltpu.VMEM((64, width), BF16), pltpu.VMEM((64, model), BF16)],
        ),
        compiler_params=params(32),
        name="project",
    )(order, idx_in, idx_out, act, grad, bank_in_t, bank_out_t)


def factor_kernel(lens, a0, a1, b1, b2, b3, out):
    slots = a0.shape[1]
    for r in range(2):
        total = (a0[r] + a1[r]) + (b1[r] + b2[r]) + b3[r]
        used = lax.broadcasted_iota(jnp.int32, (slots, 64), 0) < lens[r]
        grad = jnp.where(used, total[:, 64:128], 0.0)
        out[r] = mm3(split(grad), split(total[:, 0:64]), TN)


def factor(lens, pieces):
    return pl.pallas_call(
        factor_kernel,
        out_shape=jax.ShapeDtypeStruct((2, 64, 64), F32),
        in_specs=[SMEM] + [VMEM] * 5,
        out_specs=VMEM,
        name="factor",
    )(lens, *pieces)


def block_at(where, dx, dz):
    x = lax.rem(where[0] + (SIDE - dx), SIDE)
    z = lax.rem(where[1] + (SIDE - dz), SIDE)
    return pl.multiple_of((x * SIDE + z) * BLK, BLK)


def prior_kernel(where, g0, g1, g2, g3, prior, full, out):
    for dx, piece in enumerate((g0, g1, g2, g3)):
        for dz in range(SIDE):
            full[:, pl.ds(block_at(where, dx, dz), BLK)] = piece[:, dz * BLK : (dz + 1) * BLK]
    acc = jnp.zeros((64, BLK), F32)
    for k in range(16):
        cols = slice(k * BLK, (k + 1) * BLK)
        acc = acc + mm3(split(full[:, cols]), split(prior[:, cols]), NT)
    out[0:64, :] = acc
    own = prior[:, pl.ds(pl.multiple_of(where[2] * BLK, BLK), BLK)]
    row = lax.broadcasted_iota(jnp.int32, (BLK, BLK), 0)
    col = lax.broadcasted_iota(jnp.int32, (BLK, BLK), 1)
    out[64:72, :] = jnp.broadcast_to(jnp.sum(jnp.where(row == col, own, 0.0), axis=0, keepdims=True), (8, BLK))


def prior_image(where, pieces, prior):
    return pl.pallas_call(
        prior_kernel,
        out_shape=(
            jax.ShapeDtypeStruct((64, prior.shape[1]), F32),
            jax.ShapeDtypeStruct((72, BLK), F32),
        ),
        in_specs=[SMEM] + [VMEM] * 5,
        out_specs=(VMEM, VMEM),
        compiler_params=params(32),
        name="prior_image",
    )(where, *pieces, prior)


def rowsum(value):
    return jnp.sum(value, axis=1, keepdims=True)


def local_image(stack, cov_hi, cov_lo):
    both = mm(stack[...], cov_hi[...], NT)
    return both[0:64] + both[64:128] + mm(stack[0:64, :], cov_lo[...], NT)


def next_direction(res, direc, stack, beta, old):
    for k in range(16):
        cols = slice(k * BLK, (k + 1) * BLK)
        value = res[:, cols] + beta * old[:, cols]
        direc[:, cols] = value
        high, low = split(value)
        stack[0:64, cols] = high
        stack[64:128, cols] = low


def own_scores(stack, own_hi, own_lo):
    both = mm(stack[...], own_hi[...], NT)
    return both[0:64] + both[64:128] + mm(stack[0:64, :], own_lo[...], NT)


def first_kernel(
    where, near, far, start, image, prior,
    res, direc, rr, score, query, out, cov_hi, cov_lo, own_hi, own_lo,
    f_hi, f_lo, stack,
):
    square = jnp.zeros((64, BLK), F32)
    for part, ref in enumerate((near, far)):
        for k in range(16):
            cols = slice(k * BLK, (k + 1) * BLK)
            for half in range(2):
                rows = slice(half * 64, (half + 1) * 64)
                value = ref[rows, cols]
                square = square + value * value
                high, low = split(value)
                f_hi[part * 128 + half * 64 : part * 128 + (half + 1) * 64, cols] = high
                f_lo[part * 128 + half * 64 : part * 128 + (half + 1) * 64, cols] = low
    rollouts = 256
    diag = jnp.zeros((8, BLK), F32)
    for i in range(16):
        diag = diag + image[i, 64:72, :]
    features = prior.shape[1]
    trace = jnp.sum(diag) / 8.0 + jnp.sum(square) / rollouts
    damping = 0.1 * trace / features

    own_hi[0:8, :] = f_hi[0:8, :]
    own_hi[8:16, :] = f_hi[128:136, :]
    own_lo[0:8, :] = f_lo[0:8, :]
    own_lo[8:16, :] = f_lo[128:136, :]

    for k in range(16):
        cols = slice(k * BLK, (k + 1) * BLK)
        high, low = split(start[:, cols])
        stack[0:64, cols] = high
        stack[64:128, cols] = low
    both = mm(stack[...], f_hi[...], NT)
    q = both[0:64] + both[64:128] + mm(stack[0:64, :], f_lo[...], NT)
    q_parts = split(q * (1.0 / rollouts))
    norm = jnp.zeros((64, 1), F32)
    curve = jnp.zeros((64, 1), F32)
    for k in range(16):
        cols = slice(k * BLK, (k + 1) * BLK)
        b = start[:, cols]
        value = image[k, 0:64, :] + mm3(q_parts, (f_hi[:, cols], f_lo[:, cols]), NN) + damping * b
        res[:, cols] = value
        norm = norm + rowsum(b * b)
        curve = curve + rowsum(b * value)
    alpha = norm / curve
    fresh = jnp.zeros((64, 1), F32)
    for k in range(16):
        cols = slice(k * BLK, (k + 1) * BLK)
        value = start[:, cols] - alpha * res[:, cols]
        res[:, cols] = value
        fresh = fresh + rowsum(value * value)
    next_direction(res, direc, stack, fresh / norm, start)
    rr[...] = jnp.broadcast_to(fresh, rr.shape)
    score[:, 0:8] = alpha * q[:, 0:8]
    score[:, 8:16] = alpha * q[:, 128:136]

    first = pl.multiple_of(where[2] * BLK, BLK)
    mine = (f_hi[:, pl.ds(first, BLK)], f_lo[:, pl.ds(first, BLK)])
    row = lax.broadcasted_iota(jnp.int32, (BLK, BLK), 0)
    col = lax.broadcasted_iota(jnp.int32, (BLK, BLK), 1)
    for k in range(16):
        cols = slice(k * BLK, (k + 1) * BLK)
        value = prior[:, cols] + mm3(mine, (f_hi[:, cols], f_lo[:, cols]), TN) * (1.0 / rollouts)
        value = value + jnp.where(row + where[2] * BLK == col + k * BLK, damping, 0.0)
        high, low = split(value)
        cov_hi[:, cols] = high
        cov_lo[:, cols] = low
    out[...] = local_image(stack, cov_hi, cov_lo)
    query[...] = own_scores(stack, own_hi, own_lo)


def first_step(where, near, far, start, image, prior):
    n = prior.shape[1]
    sds = jax.ShapeDtypeStruct
    return pl.pallas_call(
        first_kernel,
        out_shape=(
            sds((64, n), F32), sds((64, n), F32), sds((64, 128), F32),
            sds((64, 16), F32), sds((64, 16), F32), sds((64, BLK), F32),
            sds((BLK, n), BF16), sds((BLK, n), BF16), sds((16, n), BF16), sds((16, n), BF16),
        ),
        in_specs=[SMEM] + [VMEM] * 5,
        out_specs=(VMEM,) * 10,
        scratch_shapes=[
            pltpu.VMEM((256, n), BF16), pltpu.VMEM((256, n), BF16), pltpu.VMEM((128, n), BF16),
        ],
        compiler_params=params(48),
        name="first_step",
    )(where, near, far, start, image, prior)


def step_kernel(
    where, g0, g1, g2, g3, res_in, direc_in, rr_in, score_in, query_in,
    cov_hi, cov_lo, own_hi, own_lo,
    res, direc, rr, score, query, out, stack, *, last,
):
    curve = jnp.zeros((64, 1), F32)
    for dx, piece in enumerate((g0, g1, g2, g3)):
        for dz in range(SIDE):
            at = pl.ds(block_at(where, dx, dz), BLK)
            curve = curve + rowsum(direc_in[:, at] * piece[:, dz * BLK : (dz + 1) * BLK])
    norm = rr_in[:, 0:1]
    alpha = norm / curve
    fresh = jnp.zeros((64, 1), F32)
    for dx, piece in enumerate((g0, g1, g2, g3)):
        for dz in range(SIDE):
            at = pl.ds(block_at(where, dx, dz), BLK)
            value = res_in[:, at] - alpha * piece[:, dz * BLK : (dz + 1) * BLK]
            res[:, at] = value
            fresh = fresh + rowsum(value * value)
    next_direction(res, direc, stack, fresh / norm, direc_in)
    rr[...] = jnp.broadcast_to(fresh, rr.shape)
    score[...] = score_in[...] + alpha * query_in[...]
    image = local_image(stack, cov_hi, cov_lo)
    query[...] = own_scores(stack, own_hi, own_lo)
    if last:
        mine = direc[:, pl.ds(pl.multiple_of(where[2] * BLK, BLK), BLK)]
        ones = jnp.ones((8, BLK), F32)
        out[0] = lax.dot_general(ones, mine * image, NT, precision=HIGHEST, preferred_element_type=F32)
        out[1] = lax.dot_general(ones, fresh * (lax.broadcasted_iota(jnp.int32, (64, BLK), 1) == 0).astype(F32), NT, precision=HIGHEST, preferred_element_type=F32)
    else:
        out[...] = image


def cg_step(where, pieces, state, cov, last):
    n = cov[0].shape[1]
    sds = jax.ShapeDtypeStruct
    return pl.pallas_call(
        functools.partial(step_kernel, last=last),
        out_shape=(
            sds((64, n), F32), sds((64, n), F32), sds((64, 128), F32),
            sds((64, 16), F32), sds((64, 16), F32),
            sds((2, 8, 64) if last else (64, BLK), F32),
        ),
        in_specs=[SMEM] + [VMEM] * 13,
        out_specs=(VMEM,) * 6,
        scratch_shapes=[pltpu.VMEM((128, n), BF16)],
        compiler_params=params(48),
        name="last_step" if last else "cg_step",
    )(where, *pieces, *state, *cov)


def finish_kernel(where, sums, norm, score, query, out):
    curve = sums[0]
    for i in range(1, 16):
        curve = curve + sums[i]
    alpha = norm[0:1, :] / curve[0:1, :]
    row = lax.broadcasted_iota(jnp.int32, (16, 16), 0)
    slot = lax.broadcasted_iota(jnp.int32, (16, 16), 1)
    core = lax.rem(slot // 8 + where[4], CORES)
    y = lax.rem(where[3] + SIDE - lax.rem(slot, 8) // 2, SIDE)
    pick = (row == core * 8 + y * 2 + lax.rem(slot, 2)).astype(F32)
    dot = functools.partial(lax.dot_general, dimension_numbers=NT, precision=HIGHEST, preferred_element_type=F32)
    out[...] = dot(pick, score[...]) + alpha * dot(pick, query[...])


def finish(where, sums, norm, score, query):
    return pl.pallas_call(
        finish_kernel,
        out_shape=jax.ShapeDtypeStruct((16, 64), F32),
        in_specs=[SMEM] + [VMEM] * 4,
        out_specs=VMEM,
        name="finish",
    )(where, sums, norm, score, query)


def gather_blocks(block):
    line = [block] + [lax.ppermute(block, "dp", along_z(d)) for d in (1, 2, 3)]
    line = jnp.concatenate(line, axis=1)
    return [line] + [lax.ppermute(line, "dp", along_x(d)) for d in (1, 2, 3)]


def per_device(
    activations, out_grads, lengths, bank_in, index_in, bank_out, index_out, prior_cov, val_grads
):
    dp = lax.axis_index("dp").astype(jnp.int32)
    tensor = lax.axis_index("tensor").astype(jnp.int32)
    y, core = tensor // CORES, tensor % CORES
    where = jnp.stack([dp // SIDE, dp % SIDE, dp, y, core])
    slot = jnp.arange(8, dtype=jnp.int32)
    line = ((y + slot // 2) % SIDE) * 2 + slot % 2

    start_pieces = gather_blocks(val_grads.T)

    banks = (bank_in.transpose(0, 2, 1), bank_out.transpose(0, 2, 1))
    theirs = project((1 - core) * 8 + line, index_in, index_out, activations, out_grads, *banks)
    from_core = lax.ppermute(theirs, "tensor", other_core())
    mine = project(core * 8 + line, index_in, index_out, activations, out_grads, *banks)
    from_y = [
        lax.ppermute(mine[2 * d : 2 * d + 2] + from_core[2 * d : 2 * d + 2], "tensor", along_y(d))
        for d in (1, 2, 3)
    ]
    lens = lax.dynamic_slice_in_dim(lengths, core * 8 + y * 2, 2)

    start, image_here = prior_image(where, start_pieces, prior_cov)
    image = lax.all_gather(image_here, "dp", axis=0)

    own = factor(lens, [mine[0:2], from_core[0:2], *from_y]).reshape(2, 4096)
    part = jnp.concatenate([own] + [lax.ppermute(own, "tensor", along_y(d)) for d in (1, 2, 3)], axis=0)
    for flip in (0, 1):
        moved = [lax.ppermute(part, ("dp", "tensor"), crossed(d, flip)) for d in (1, 2, 3)]
        part = jnp.concatenate([part] + moved, axis=0)
    far = lax.ppermute(part, "tensor", other_core())

    first = first_step(where, part, far, start, image, prior_cov)
    state, out, cov = first[0:5], first[5], first[6:10]
    for iteration in range(1, ITERS - 1):
        pieces = gather_blocks(out)
        *state, out = cg_step(where, pieces, state, cov, iteration + 2 == ITERS)
    sums = lax.all_to_all(jnp.broadcast_to(out[0], (16, 8, 64)), "dp", 0, 0)
    return finish(where, sums, out[1], state[3], state[4])


def solution(mesh):
    return jax.shard_map(
        per_device,
        mesh=mesh,
        in_specs=(
            P("dp", None, "tensor"),
            P("dp", None, "tensor"),
            P("dp"),
            P(),
            P("tensor"),
            P(),
            P("tensor"),
            P("dp", None),
            P("dp", "tensor"),
        ),
        out_specs=P("dp", "tensor"),
        check_vma=False,
    )
```

time: 903 us -> 292 us (0.32)
  blocking collectives: 445 us -> 13.7 us
  waiting for transfers between devices: 364 us -> 110 us
  starting transfers between devices: 0.56 us -> 69 us
  matrix products: 64.7 us -> 0 us
  Pallas kernels: 0 us -> 47.9 us
  local copies, waits for them, and re-layouts: 6.89 us -> 35.2 us
    psum x12 -> x0, blocking collectives: 445 us -> none  [the longest x5 191 us: per_device(): curvature = lax.psum(jnp.sum(direction * image, axis=0), 'dp')]
    all_gather x8 -> x1, waiting for transfers between devices: 295 us -> 33.7 us  [per_device(): image = lax.all_gather(image_here, 'dp', axis=0)]
    ppermute x0 -> x44, waiting for transfers between devices: none -> 76.4 us  [the longest x15 50.9 us: gather_blocks(): return [line] + [lax.ppermute(line, 'dp', along_x(d)) for d in (1, 2, 3)]]
    ppermute x0 -> x44, starting transfers between devices: none -> 69 us  [the longest x15 26.3 us: gather_blocks(): line = [block] + [lax.ppermute(block, 'dp', along_z(d)) for d in (1, 2, 3)]]
    psum x1 -> x0, waiting for transfers between devices: 68.2 us -> none  [per_device(): summed = lax.psum(jnp.concatenate((grad_low, act_low), axis=2), 'tensor')]
    dot_general x13 -> x0, matrix products: 64.7 us -> none  [the longest x6 39.3 us: per_device(): jnp.dot(contract_columns, contract_block_rows, precision=HIGH)]
    pallas_call x0 -> x10, Pallas kernels: none -> 47.9 us  [the longest x4 19.1 us: cg_step(): pl.pallas_call(functools.partial(step_kernel, last=last), out_shape=(sds(...]
    unnamed x22 -> x58, local copies, waits for them, and re-layouts: 4.47 us -> 24.3 us
  transfers between devices with their start and end apart: 9 -> 45, of which waited for: 8 -> 28; matrix products, arithmetic and copies ran while one was open for 1% -> 3% of each run, Pallas kernels for 0% -> 3%
where the time goes in v1:
time: 292 us; the launch traced here: 291 us
  waiting for transfers between devices  110 us (38%)
  starting transfers between devices  69 us (24%)
  Pallas kernels  47.9 us (16%)
  local copies, waits for them, and re-layouts  35.2 us (12%)
  blocking collectives  13.7 us (5%)
  between operations  13.7 us (5%)
    ppermute x15, waiting for transfers between devices, gather_blocks(): return [line] + [lax.ppermute(line, 'dp', along_x(d)) for d in (1, 2, 3)]  50.9 us
    all_gather x1, waiting for transfers between devices, per_device(): image = lax.all_gather(image_here, 'dp', axis=0)  33.7 us
    ppermute x15, starting transfers between devices, gather_blocks(): line = [block] + [lax.ppermute(block, 'dp', along_z(d)) for d in (1, 2, 3)]  26.3 us
    unnamed x58, local copies, waits for them, and re-layouts  24.3 us
    ppermute x15, starting transfers between devices, gather_blocks(): return [line] + [lax.ppermute(line, 'dp', along_x(d)) for d in (1, 2, 3)]  22 us
    pallas_call x4, Pallas kernels, cg_step(): pl.pallas_call(functools.partial(step_kernel, last=last), out_shape=(sds(...  19.1 us
    all_to_all x1, blocking collectives, per_device(): sums = lax.all_to_all(jnp.broadcast_to(out[0], (16, 8, 64)), 'dp', 0, 0)  13.7 us
    ppermute x15, waiting for transfers between devices, gather_blocks(): line = [block] + [lax.ppermute(block, 'dp', along_z(d)) for d in (1, 2, 3)]  12.1 us
  transfers between devices with their start and end apart: 45, of which 28 were waited for; matrix products, arithmetic and copies ran while one was open for 3% of the time, Pallas kernels for 3%

profile of v1, /device:TPU:0, one launch (start us, length us, event | category | flops | bytes accessed | tf_op | source)
XLA Modules:
  0.0 291.3 jit_solution(9090343369533988513)
XLA Ops:
  6.6 5.2 %copy-done = bf16[16,256,1792]{2,1,0:T(8,128)(2,1)S(1)} copy-done((bf16[16,256,1792]{2,1,0:T(8,128)(2,1)S(1)}, bf16[16,256,1792]{2,1,0:T(8,128)(2,1)}, u32[]{:S(2)}) %copy-start) | copy-done | bytes 14680088
  17.1 4.8 %project.3 = f32[8,256,128]{2,1,0:T(8,128)S(1)} custom-call(s32[8]{0:T(128)S(1)} %broadcast_add_fusion.order, s32[14]{0:T(128)S(1)} %copy-done.13, s32[4]{0:T(128)S(1)} %copy-done.15, bf16[16,256,1792]{2,1,0:T(8,128)(2,1)S(1)} %copy-done, bf16[16,256,512]{2,1,0:T(8,128)(2,1)S(1)} %copy-done.3, bf16[16,64,128]{2,1,0:T(8,128)(2,1)S(1)} %bitcast.14, ...), custom_call_target="tpu_custom_call" | custom-call | tf_op jit(solution)/shard_map/project/pallas_call | solution.py:83
  22.1 5.2 %copy-done.1 = bf16[16,256,1792]{2,1,0:T(8,128)(2,1)S(1)} copy-done((bf16[16,256,1792]{2,1,0:T(8,128)(2,1)S(1)}, bf16[16,256,1792]{2,1,0:T(8,128)(2,1)}, u32[]{:S(2)}) %copy-start.1) | copy-done | bytes 14680088
  29.5 4.9 %project.2 = f32[8,256,128]{2,1,0:T(8,128)S(1)} custom-call(s32[8]{0:T(128)S(1)} %fusion.4.order, s32[14]{0:T(128)S(1)} %copy-done.14, s32[4]{0:T(128)S(1)} %copy-done.16, bf16[16,256,1792]{2,1,0:T(8,128)(2,1)S(1)} %copy-done.1, bf16[16,256,512]{2,1,0:T(8,128)(2,1)S(1)} %copy-done.4, bf16[16,64,128]{2,1,0:T(8,128)(2,1)S(1)} %bitcast.15, ...), custom_call_target="tpu_custom_call" | custom-call | tf_op jit(solution)/shard_map/project/pallas_call | solution.py:83
  37.0 2.9 collective-permute-start.2
  41.8 3.6 %collective-permute-done.1.b1 = f32[2,256,128]{2,1,0:T(8,128)S(1)} collective-permute-done((f32[2,256,128]{2,1,0:T(8,128)S(1)}, f32[2,256,128]{2,1,0:T(8,128)S(1)}, u32[]{:S(2)}, u32[]{:S(2)}) %collective-permute-start.1) | collective-permute-done | bytes 262176 | tf_op jit(solution)/shard_map/ppermute | solution.py:372
  45.4 6.8 %collective-permute-done.2.b2 = f32[2,256,128]{2,1,0:T(8,128)S(1)} collective-permute-done((f32[2,256,128]{2,1,0:T(8,128)S(1)}, f32[2,256,128]{2,1,0:T(8,128)S(1)}, u32[]{:S(2)}, u32[]{:S(2)}) %collective-permute-start.2) | collective-permute-done | bytes 262176 | tf_op jit(solution)/shard_map/ppermute | solution.py:372
  63.3 3.6 %collective-permute-start.15 = (f32[64,256]{1,0:T(8,128)S(1)}, f32[64,256]{1,0:T(8,128)S(1)}, u32[]{:S(2)}, u32[]{:S(2)}) collective-permute-start(f32[64,256]{1,0:T(8,128)S(1)} %bitcast.19), channel_id=1, source_target_pairs={{0,16},{8,24},{16,0},{24,8},{32,48},{40,56},{48,32},{56,40},{64,80... | collective-permute-start | bytes 196616 | tf_op jit(solution)/shard_map/ppermute | solution.py:350
  78.2 2.7 collective-permute-start.11
  82.9 2.7 collective-permute-start.19
  85.7 12.2 %collective-permute-done.18.g2 = f32[64,1024]{1,0:T(8,128)S(1)} collective-permute-done((f32[64,1024]{1,0:T(8,128)S(1)}, f32[64,1024]{1,0:T(8,128)S(1)}, u32[]{:S(2)}, u32[]{:S(2)}) %collective-permute-start.18) | collective-permute-done | bytes 262176 | tf_op jit(solution)/shard_map/ppermute | solution.py:352
  97.9 5.4 %collective-permute-done.19.g3 = f32[64,1024]{1,0:T(8,128)S(1)} collective-permute-done((f32[64,1024]{1,0:T(8,128)S(1)}, f32[64,1024]{1,0:T(8,128)S(1)}, u32[]{:S(2)}, u32[]{:S(2)}) %collective-permute-start.19) | collective-permute-done | bytes 262176 | tf_op jit(solution)/shard_map/ppermute | solution.py:352
  105.5 3.3 %prior_image.1 = (f32[64,4096]{1,0:T(8,128)S(1)}, f32[72,256]{1,0:T(8,128)}) custom-call(s32[5]{0:T(128)S(1)} %stack.23.where, f32[64,1024]{1,0:T(8,128)S(1)} %pad_maximum_fusion.g0, f32[64,1024]{1,0:T(8,128)S(1)} %collective-permute-done.17.g1, f32[64,1024]{1,0:T(8,128)S(1)} %collective-permute-done.18.g2, f32[64,1024]{1,0:T(8,128)S(1)} %collective-permute-done.19.g3, ...), custom_call_target="tpu_custom_call" | custom-call | tf_op jit(solution)/shard_map/prior_image/pallas_call | solution.py:144
  108.8 8.0 %concatenate.28.near = f32[128,4096]{1,0:T(8,128)} concatenate(f32[2,4096]{1,0:T(2,128)S(1)} %reshape.3, f32[2,4096]{1,0:T(2,128)S(1)} %collective-permute-done.4, f32[2,4096]{1,0:T(2,128)S(1)} %collective-permute-done.5, f32[2,4096]{1,0:T(2,128)S(1)} %collective-permute-done.6, f32[8,4096]{1,0:T(8,128)S(1)} %collective-permute-done.7, f32[8,4096]{1,0:T(8,128)S(1)} %collective-permute-done.8, ...), dimensions={0} | concatenate | bytes 4194304 | tf_op jit(solution)/shard_map/concatenate | solution.py:384
  116.9 33.7 %all-gather.3.cloned.1.call-done = f32[1152,256]{1,0:T(8,128)} async-done(((f32[72,256]{1,0:T(8,128)}), f32[1152,256]{1,0:T(8,128)}) %all-gather.3.cloned.1.call-update) | async-done | bytes 1179664 | tf_op jit(solution)/shard_map/all_gather | solution.py:378
  151.9 11.9 %first_step.1 = (f32[64,4096]{1,0:T(8,128)S(1)}, f32[64,4096]{1,0:T(8,128)S(1)}, f32[64,128]{1,0:T(8,128)S(1)}, f32[64,16]{1,0:T(8,128)S(1)}, f32[64,16]{1,0:T(8...) custom-call(s32[5]{0:T(128)S(1)} %stack.23.where, ...), custom_call_target="tpu_custom_call" | custom-call | tf_op jit(solution)/shard_map/first_step/pallas_call | solution.py:257
  165.1 2.7 collective-permute-start.21
  176.2 8.4 %collective-permute-done.23.g1 = f32[64,1024]{1,0:T(8,128)S(1)} collective-permute-done((f32[64,1024]{1,0:T(8,128)S(1)}, f32[64,1024]{1,0:T(8,128)S(1)}, u32[]{:S(2)}, u32[]{:S(2)}) %collective-permute-start.23) | collective-permute-done | bytes 262176 | tf_op jit(solution)/shard_map/ppermute | solution.py:352
  185.2 4.6 %cg_step.3 = (f32[64,4096]{1,0:T(8,128)S(1)}, f32[64,4096]{1,0:T(8,128)S(1)}, f32[64,128]{1,0:T(8,128)S(1)}, f32[64,16]{1,0:T(8,128)S(1)}, f32[64,16]{1,0:T(8,128)S(1)}, /*index=5*/f32[64,256]{1,0:T(8,128)S(1)}) custom-call(s32[5]{0:T(128)S(1)} %stack.23.where, f32[64,1024]{1,0:T(8,128)S(1)} %constant_dynamic-update-slice_fusion.g0, ...), custom_call_target="tpu_custom_call" | custom-call | tf_op jit(solution)/shard_map/cg_step/pallas_call | solution.py:310
  190.2 2.7 collective-permute-start.27
  202.1 5.2 %collective-permute-done.29.g1 = f32[64,1024]{1,0:T(8,128)S(1)} collective-permute-done((f32[64,1024]{1,0:T(8,128)S(1)}, f32[64,1024]{1,0:T(8,128)S(1)}, u32[]{:S(2)}, u32[]{:S(2)}) %collective-permute-start.29) | collective-permute-done | bytes 262176 | tf_op jit(solution)/shard_map/ppermute | solution.py:352
  207.3 2.8 collective-permute-done.30.g2
  210.1 4.6 %cg_step.4 = (f32[64,4096]{1,0:T(8,128)S(1)}, f32[64,4096]{1,0:T(8,128)S(1)}, f32[64,128]{1,0:T(8,128)S(1)}, f32[64,16]{1,0:T(8,128)S(1)}, f32[64,16]{1,0:T(8,128)S(1)}, /*index=5*/f32[64,256]{1,0:T(8,128)S(1)}) custom-call(s32[5]{0:T(128)S(1)} %stack.23.where, f32[64,1024]{1,0:T(8,128)S(1)} %constant_dynamic-update-slice_fusion.4.g0, ...), custom_call_target="tpu_custom_call" | custom-call | tf_op jit(solution)/shard_map/cg_step/pallas_call | solution.py:310
  216.5 2.9 collective-permute-start.33
  223.7 3.6 %collective-permute-start.36 = (f32[64,1024]{1,0:T(8,128)S(1)}, f32[64,1024]{1,0:T(8,128)S(1)}, u32[]{:S(2)}, u32[]{:S(2)}) collective-permute-start(f32[64,1024]{1,0:T(8,128)S(1)} %constant_dynamic-update-slice_fusion.8.g0), channel_id=1, source_target_pairs={{0,64},{8,72},{16,80},{24,88},{32,96},{40,104},{48,112},{56,120},{... | collective-permute-start | bytes 786440 | tf_op jit(solution)/shard_map/ppermute | solution.py:352
  227.2 6.0 %collective-permute-done.35.g1 = f32[64,1024]{1,0:T(8,128)S(1)} collective-permute-done((f32[64,1024]{1,0:T(8,128)S(1)}, f32[64,1024]{1,0:T(8,128)S(1)}, u32[]{:S(2)}, u32[]{:S(2)}) %collective-permute-start.35) | collective-permute-done | bytes 262176 | tf_op jit(solution)/shard_map/ppermute | solution.py:352
  233.2 2.8 collective-permute-done.36.g2
  236.0 4.6 %cg_step.5 = (f32[64,4096]{1,0:T(8,128)S(1)}, f32[64,4096]{1,0:T(8,128)S(1)}, f32[64,128]{1,0:T(8,128)S(1)}, f32[64,16]{1,0:T(8,128)S(1)}, f32[64,16]{1,0:T(8,128)S(1)}, /*index=5*/f32[64,256]{1,0:T(8,128)S(1)}) custom-call(s32[5]{0:T(128)S(1)} %stack.23.where, f32[64,1024]{1,0:T(8,128)S(1)} %constant_dynamic-update-slice_fusion.8.g0, ...), custom_call_target="tpu_custom_call" | custom-call | tf_op jit(solution)/shard_map/cg_step/pallas_call | solution.py:310
  252.5 4.7 %collective-permute-done.41.g1 = f32[64,1024]{1,0:T(8,128)S(1)} collective-permute-done((f32[64,1024]{1,0:T(8,128)S(1)}, f32[64,1024]{1,0:T(8,128)S(1)}, u32[]{:S(2)}, u32[]{:S(2)}) %collective-permute-start.41) | collective-permute-done | bytes 262176 | tf_op jit(solution)/shard_map/ppermute | solution.py:352
  257.1 2.8 collective-permute-done.42.g2
  260.0 5.3 %last_step.1 = (f32[64,4096]{1,0:T(8,128)}, f32[64,4096]{1,0:T(8,128)}, f32[64,128]{1,0:T(8,128)}, f32[64,16]{1,0:T(8,128)S(1)}, f32[64,16]{1,0:T(8,128)S(1)}, /*index=5*/f32[2,8,64]{2,1,0:T(8,128)S(1)}) custom-call(s32[5]{0:T(128)S(1)} %stack.23.where, f32[64,1024]{1,0:T(8,128)S(1)} %constant_dynamic-update-slice_fusion.12.g0, ...), custom_call_target="tpu_custom_call" | custom-call | tf_op jit(solution)/shard_map/last_step/pallas_call | solution.py:310
  267.2 13.7 %all_to_all.5 = f32[16,1,512]{2,1,0:T(1,128)S(1)} all-to-all(f32[16,1,512]{2,1,0:T(1,128)S(1)} %reshape.5), channel_id=1, replica_groups=mesh['dp'=16,'tensor'=8] {'dp'}, dimensions={0} | all-to-all | bytes 65536 | tf_op jit(solution)/shard_map/all_to_all | solution.py:392
  (146 shorter events, 83.6 us)
Async XLA Ops:
  6.5 144.1 %all-gather.3.cloned.1.call-start = ((), (), s32[]{:S(2)}) async-start(), calls=%async_computation.1 | async-start | bytes 1253376 | tf_op jit(solution)/shard_map/all_gather | solution.py:378
  22.0 12.4 %collective-permute-start = (f32[8,256,128]{2,1,0:T(8,128)S(1)}, f32[8,256,128]{2,1,0:T(8,128)S(1)}, u32[]{:S(2)}, u32[]{:S(2)}) collective-permute-start(f32[8,256,128]{2,1,0:T(8,128)S(1)} %project.3), channel_id=1, source_target_pairs={{0,1},{1,0},{2,3},{3,2},{4,5},{5,4},{6,7},{7,6},{8,9},{9,8},{10,11... | collective-permute-start | bytes 3145736 | tf_op jit(solution)/shard_map/ppermute | solution.py:369
  35.3 10.1 %collective-permute-start.1 = (f32[2,256,128]{2,1,0:T(8,128)S(1)}, f32[2,256,128]{2,1,0:T(8,128)S(1)}, u32[]{:S(2)}, u32[]{:S(2)}) collective-permute-start(f32[2,256,128]{2,1,0:T(8,128)S(1)} %get-tuple-element.73), channel_id=1, source_target_pairs={{0,2},{1,3},{2,4},{3,5},{4,6},{5,7},{6,0},{7,1},{8,10},{9,11},{10,... | collective-permute-start | bytes 786440 | tf_op jit(solution)/shard_map/ppermute | solution.py:372
  37.0 15.2 %collective-permute-start.2 = (f32[2,256,128]{2,1,0:T(8,128)S(1)}, f32[2,256,128]{2,1,0:T(8,128)S(1)}, u32[]{:S(2)}, u32[]{:S(2)}) collective-permute-start(f32[2,256,128]{2,1,0:T(8,128)S(1)} %get-tuple-element.72), channel_id=1, source_target_pairs={{0,4},{1,5},{2,6},{3,7},{4,0},{5,1},{6,2},{7,3},{8,12},{9,13},{10,... | collective-permute-start | bytes 786440 | tf_op jit(solution)/shard_map/ppermute | solution.py:372
  39.9 12.3 %collective-permute-start.3 = (f32[2,256,128]{2,1,0:T(8,128)S(1)}, f32[2,256,128]{2,1,0:T(8,128)S(1)}, u32[]{:S(2)}, u32[]{:S(2)}) collective-permute-start(f32[2,256,128]{2,1,0:T(8,128)S(1)} %get-tuple-element.71), channel_id=1, source_target_pairs={{0,6},{1,7},{2,0},{3,1},{4,2},{5,3},{6,4},{7,5},{8,14},{9,15},{10,... | collective-permute-start | bytes 786440 | tf_op jit(solution)/shard_map/ppermute | solution.py:372
  56.2 10.7 %collective-permute-start.4 = (f32[2,4096]{1,0:T(2,128)S(1)}, f32[2,4096]{1,0:T(2,128)S(1)}, u32[]{:S(2)}, u32[]{:S(2)}) collective-permute-start(f32[2,4096]{1,0:T(2,128)S(1)} %reshape.3), channel_id=1, source_target_pairs={{0,2},{1,3},{2,4},{3,5},{4,6},{5,7},{6,0},{7,1},{8,10},{9,11},{10,... | collective-permute-start | bytes 98312 | tf_op jit(solution)/shard_map/ppermute | solution.py:381
  57.3 10.6 %collective-permute-start.5 = (f32[2,4096]{1,0:T(2,128)S(1)}, f32[2,4096]{1,0:T(2,128)S(1)}, u32[]{:S(2)}, u32[]{:S(2)}) collective-permute-start(f32[2,4096]{1,0:T(2,128)S(1)} %reshape.3), channel_id=1, source_target_pairs={{0,4},{1,5},{2,6},{3,7},{4,0},{5,1},{6,2},{7,3},{8,12},{9,13},{10,... | collective-permute-start | bytes 98312 | tf_op jit(solution)/shard_map/ppermute | solution.py:381
  59.7 8.2 %collective-permute-start.6 = (f32[2,4096]{1,0:T(2,128)S(1)}, f32[2,4096]{1,0:T(2,128)S(1)}, u32[]{:S(2)}, u32[]{:S(2)}) collective-permute-start(f32[2,4096]{1,0:T(2,128)S(1)} %reshape.3), channel_id=1, source_target_pairs={{0,6},{1,7},{2,0},{3,1},{4,2},{5,3},{6,4},{7,5},{8,14},{9,15},{10,... | collective-permute-start | bytes 98312 | tf_op jit(solution)/shard_map/ppermute | solution.py:381
  61.4 8.1 %collective-permute-start.14 = (f32[64,256]{1,0:T(8,128)S(1)}, f32[64,256]{1,0:T(8,128)S(1)}, u32[]{:S(2)}, u32[]{:S(2)}) collective-permute-start(f32[64,256]{1,0:T(8,128)S(1)} %bitcast.18), channel_id=1, source_target_pairs={{0,8},{8,16},{16,24},{24,0},{32,40},{40,48},{48,56},{56,32},{64,72... | collective-permute-start | bytes 196616 | tf_op jit(solution)/shard_map/ppermute | solution.py:350
  63.3 8.5 %collective-permute-start.15 = (f32[64,256]{1,0:T(8,128)S(1)}, f32[64,256]{1,0:T(8,128)S(1)}, u32[]{:S(2)}, u32[]{:S(2)}) collective-permute-start(f32[64,256]{1,0:T(8,128)S(1)} %bitcast.19), channel_id=1, source_target_pairs={{0,16},{8,24},{16,0},{24,8},{32,48},{40,56},{48,32},{56,40},{64,80... | collective-permute-start | bytes 196616 | tf_op jit(solution)/shard_map/ppermute | solution.py:350
  68.0 6.3 %collective-permute-start.7 = (f32[8,4096]{1,0:T(8,128)S(1)}, f32[8,4096]{1,0:T(8,128)S(1)}, u32[]{:S(2)}, u32[]{:S(2)}) collective-permute-start(f32[8,4096]{1,0:T(8,128)S(1)} %pad_maximum_fusion.1), channel_id=1, source_target_pairs={{0,8},{1,33},{2,10},{3,35},{4,12},{5,37},{6,14},{7,39},{8,16},{9,4... | collective-permute-start | bytes 393224 | tf_op jit(solution)/shard_map/ppermute | solution.py:383
  69.1 6.6 %collective-permute-start.8 = (f32[8,4096]{1,0:T(8,128)S(1)}, f32[8,4096]{1,0:T(8,128)S(1)}, u32[]{:S(2)}, u32[]{:S(2)}) collective-permute-start(f32[8,4096]{1,0:T(8,128)S(1)} %pad_maximum_fusion.1), channel_id=1, source_target_pairs={{0,16},{1,65},{2,18},{3,67},{4,20},{5,69},{6,22},{7,71},{8,24},{9,... | collective-permute-start | bytes 393224 | tf_op jit(solution)/shard_map/ppermute | solution.py:383
  69.5 7.0 %collective-permute-start.9 = (f32[8,4096]{1,0:T(8,128)S(1)}, f32[8,4096]{1,0:T(8,128)S(1)}, u32[]{:S(2)}, u32[]{:S(2)}) collective-permute-start(f32[8,4096]{1,0:T(8,128)S(1)} %pad_maximum_fusion.1), channel_id=1, source_target_pairs={{0,24},{1,97},{2,26},{3,99},{4,28},{5,101},{6,30},{7,103},{8,0},{9... | collective-permute-start | bytes 393224 | tf_op jit(solution)/shard_map/ppermute | solution.py:383
  71.9 11.0 %collective-permute-start.17 = (f32[64,1024]{1,0:T(8,128)S(1)}, f32[64,1024]{1,0:T(8,128)S(1)}, u32[]{:S(2)}, u32[]{:S(2)}) collective-permute-start(f32[64,1024]{1,0:T(8,128)S(1)} %pad_maximum_fusion.g0), channel_id=1, source_target_pairs={{0,32},{8,40},{16,48},{24,56},{32,64},{40,72},{48,80},{56,88},{64,... | collective-permute-start | bytes 786440 | tf_op jit(solution)/shard_map/ppermute | solution.py:352
  76.6 32.2 %collective-permute-start.10 = (f32[32,4096]{1,0:T(8,128)S(1)}, f32[32,4096]{1,0:T(8,128)}, u32[]{:S(2)}, u32[]{:S(2)}) collective-permute-start(f32[32,4096]{1,0:T(8,128)S(1)} %concatenate.27), channel_id=1, source_target_pairs={{0,32},{1,9},{2,34},{3,11},{4,36},{5,13},{6,38},{7,15},{8,40},{9,1... | collective-permute-start | bytes 1572872 | tf_op jit(solution)/shard_map/ppermute | solution.py:383
  78.2 30.6 %collective-permute-start.11 = (f32[32,4096]{1,0:T(8,128)S(1)}, f32[32,4096]{1,0:T(8,128)}, u32[]{:S(2)}, u32[]{:S(2)}) collective-permute-start(f32[32,4096]{1,0:T(8,128)S(1)} %concatenate.27), channel_id=1, source_target_pairs={{0,64},{1,17},{2,66},{3,19},{4,68},{5,21},{6,70},{7,23},{8,72},{9,... | collective-permute-start | bytes 1572872 | tf_op jit(solution)/shard_map/ppermute | solution.py:383
  80.9 27.9 %collective-permute-start.12 = (f32[32,4096]{1,0:T(8,128)S(1)}, f32[32,4096]{1,0:T(8,128)}, u32[]{:S(2)}, u32[]{:S(2)}) collective-permute-start(f32[32,4096]{1,0:T(8,128)S(1)} %concatenate.27), channel_id=1, source_target_pairs={{0,96},{1,25},{2,98},{3,27},{4,100},{5,29},{6,102},{7,31},{8,104},... | collective-permute-start | bytes 1572872 | tf_op jit(solution)/shard_map/ppermute | solution.py:383
  82.4 15.6 %collective-permute-start.18 = (f32[64,1024]{1,0:T(8,128)S(1)}, f32[64,1024]{1,0:T(8,128)S(1)}, u32[]{:S(2)}, u32[]{:S(2)}) collective-permute-start(f32[64,1024]{1,0:T(8,128)S(1)} %pad_maximum_fusion.g0), channel_id=1, source_target_pairs={{0,64},{8,72},{16,80},{24,88},{32,96},{40,104},{48,112},{56,120},{... | collective-permute-start | bytes 786440 | tf_op jit(solution)/shard_map/ppermute | solution.py:352
  82.9 20.5 %collective-permute-start.19 = (f32[64,1024]{1,0:T(8,128)S(1)}, f32[64,1024]{1,0:T(8,128)S(1)}, u32[]{:S(2)}, u32[]{:S(2)}) collective-permute-start(f32[64,1024]{1,0:T(8,128)S(1)} %pad_maximum_fusion.g0), channel_id=1, source_target_pairs={{0,96},{8,104},{16,112},{24,120},{32,0},{40,8},{48,16},{56,24},{64... | collective-permute-start | bytes 786440 | tf_op jit(solution)/shard_map/ppermute | solution.py:352
  116.9 33.8 %collective-permute-start.13 = (f32[128,4096]{1,0:T(8,128)}, f32[128,4096]{1,0:T(8,128)}, u32[]{:S(2)}, u32[]{:S(2)}) collective-permute-start(f32[128,4096]{1,0:T(8,128)} %concatenate.28.near), channel_id=1, source_target_pairs={{0,1},{1,0},{2,3},{3,2},{4,5},{5,4},{6,7},{7,6},{8,9},{9,8},{10,11... | collective-permute-start | bytes 6291464 | tf_op jit(solution)/shard_map/ppermute | solution.py:385
  172.0 12.5 %collective-permute-start.23 = (f32[64,1024]{1,0:T(8,128)S(1)}, f32[64,1024]{1,0:T(8,128)S(1)}, u32[]{:S(2)}, u32[]{:S(2)}) collective-permute-start(f32[64,1024]{1,0:T(8,128)S(1)} %constant_dynamic-update-slice_fusion.g0), channel_id=1, source_target_pairs={{0,32},{8,40},{16,48},{24,56},{32,64},{40,72},{48,80},{56,88},{64,... | collective-permute-start | bytes 786440 | tf_op jit(solution)/shard_map/ppermute | solution.py:352
  172.3 12.3 %collective-permute-start.24 = (f32[64,1024]{1,0:T(8,128)S(1)}, f32[64,1024]{1,0:T(8,128)S(1)}, u32[]{:S(2)}, u32[]{:S(2)}) collective-permute-start(f32[64,1024]{1,0:T(8,128)S(1)} %constant_dynamic-update-slice_fusion.g0), channel_id=1, source_target_pairs={{0,64},{8,72},{16,80},{24,88},{32,96},{40,104},{48,112},{56,120},{... | collective-permute-start | bytes 786440 | tf_op jit(solution)/shard_map/ppermute | solution.py:352
  174.8 10.4 %collective-permute-start.25 = (f32[64,1024]{1,0:T(8,128)S(1)}, f32[64,1024]{1,0:T(8,128)S(1)}, u32[]{:S(2)}, u32[]{:S(2)}) collective-permute-start(f32[64,1024]{1,0:T(8,128)S(1)} %constant_dynamic-update-slice_fusion.g0), channel_id=1, source_target_pairs={{0,96},{8,104},{16,112},{24,120},{32,0},{40,8},{48,16},{56,24},{64... | collective-permute-start | bytes 786440 | tf_op jit(solution)/shard_map/ppermute | solution.py:352
  197.2 10.1 %collective-permute-start.29 = (f32[64,1024]{1,0:T(8,128)S(1)}, f32[64,1024]{1,0:T(8,128)S(1)}, u32[]{:S(2)}, u32[]{:S(2)}) collective-permute-start(f32[64,1024]{1,0:T(8,128)S(1)} %constant_dynamic-update-slice_fusion.4.g0), channel_id=1, source_target_pairs={{0,32},{8,40},{16,48},{24,56},{32,64},{40,72},{48,80},{56,88},{64,... | collective-permute-start | bytes 786440 | tf_op jit(solution)/shard_map/ppermute | solution.py:352
  198.8 11.3 %collective-permute-start.30 = (f32[64,1024]{1,0:T(8,128)S(1)}, f32[64,1024]{1,0:T(8,128)S(1)}, u32[]{:S(2)}, u32[]{:S(2)}) collective-permute-start(f32[64,1024]{1,0:T(8,128)S(1)} %constant_dynamic-update-slice_fusion.4.g0), channel_id=1, source_target_pairs={{0,64},{8,72},{16,80},{24,88},{32,96},{40,104},{48,112},{56,120},{... | collective-permute-start | bytes 786440 | tf_op jit(solution)/shard_map/ppermute | solution.py:352
  201.3 8.8 %collective-permute-start.31 = (f32[64,1024]{1,0:T(8,128)S(1)}, f32[64,1024]{1,0:T(8,128)S(1)}, u32[]{:S(2)}, u32[]{:S(2)}) collective-permute-start(f32[64,1024]{1,0:T(8,128)S(1)} %constant_dynamic-update-slice_fusion.4.g0), channel_id=1, source_target_pairs={{0,96},{8,104},{16,112},{24,120},{32,0},{40,8},{48,16},{56,24},{64... | collective-permute-start | bytes 786440 | tf_op jit(solution)/shard_map/ppermute | solution.py:352
  223.6 9.6 %collective-permute-start.35 = (f32[64,1024]{1,0:T(8,128)S(1)}, f32[64,1024]{1,0:T(8,128)S(1)}, u32[]{:S(2)}, u32[]{:S(2)}) collective-permute-start(f32[64,1024]{1,0:T(8,128)S(1)} %constant_dynamic-update-slice_fusion.8.g0), channel_id=1, source_target_pairs={{0,32},{8,40},{16,48},{24,56},{32,64},{40,72},{48,80},{56,88},{64,... | collective-permute-start | bytes 786440 | tf_op jit(solution)/shard_map/ppermute | solution.py:352
  223.7 12.3 %collective-permute-start.36 = (f32[64,1024]{1,0:T(8,128)S(1)}, f32[64,1024]{1,0:T(8,128)S(1)}, u32[]{:S(2)}, u32[]{:S(2)}) collective-permute-start(f32[64,1024]{1,0:T(8,128)S(1)} %constant_dynamic-update-slice_fusion.8.g0), channel_id=1, source_target_pairs={{0,64},{8,72},{16,80},{24,88},{32,96},{40,104},{48,112},{56,120},{... | collective-permute-start | bytes 786440 | tf_op jit(solution)/shard_map/ppermute | solution.py:352
  227.2 8.8 %collective-permute-start.37 = (f32[64,1024]{1,0:T(8,128)S(1)}, f32[64,1024]{1,0:T(8,128)S(1)}, u32[]{:S(2)}, u32[]{:S(2)}) collective-permute-start(f32[64,1024]{1,0:T(8,128)S(1)} %constant_dynamic-update-slice_fusion.8.g0), channel_id=1, source_target_pairs={{0,96},{8,104},{16,112},{24,120},{32,0},{40,8},{48,16},{56,24},{64... | collective-permute-start | bytes 786440 | tf_op jit(solution)/shard_map/ppermute | solution.py:352
  247.9 9.2 %collective-permute-start.41 = (f32[64,1024]{1,0:T(8,128)S(1)}, f32[64,1024]{1,0:T(8,128)S(1)}, u32[]{:S(2)}, u32[]{:S(2)}) collective-permute-start(f32[64,1024]{1,0:T(8,128)S(1)} %constant_dynamic-update-slice_fusion.12.g0), channel_id=1, source_target_pairs={{0,32},{8,40},{16,48},{24,56},{32,64},{40,72},{48,80},{56,88},{64,... | collective-permute-start | bytes 786440 | tf_op jit(solution)/shard_map/ppermute | solution.py:352
  249.1 10.8 %collective-permute-start.42 = (f32[64,1024]{1,0:T(8,128)S(1)}, f32[64,1024]{1,0:T(8,128)S(1)}, u32[]{:S(2)}, u32[]{:S(2)}) collective-permute-start(f32[64,1024]{1,0:T(8,128)S(1)} %constant_dynamic-update-slice_fusion.12.g0), channel_id=1, source_target_pairs={{0,64},{8,72},{16,80},{24,88},{32,96},{40,104},{48,112},{56,120},{... | collective-permute-start | bytes 786440 | tf_op jit(solution)/shard_map/ppermute | solution.py:352
  251.6 8.4 %collective-permute-start.43 = (f32[64,1024]{1,0:T(8,128)S(1)}, f32[64,1024]{1,0:T(8,128)S(1)}, u32[]{:S(2)}, u32[]{:S(2)}) collective-permute-start(f32[64,1024]{1,0:T(8,128)S(1)} %constant_dynamic-update-slice_fusion.12.g0), channel_id=1, source_target_pairs={{0,96},{8,104},{16,112},{24,120},{32,0},{40,8},{48,16},{56,24},{64... | collective-permute-start | bytes 786440 | tf_op jit(solution)/shard_map/ppermute | solution.py:352
  (35 other events, 326.3 us)
Sparse Core Ops, SparseCore 0:
  108.9 41.6 all-gather.2

commit v2 on v1

v2 whole, which is shorter than its diff:
```python
import functools

import jax
import jax.numpy as jnp
from jax import lax
from jax.experimental import pallas as pl
from jax.experimental.pallas import tpu as pltpu
from jax.sharding import PartitionSpec as P

ITERS = 6
F32 = jnp.float32
BF16 = jnp.bfloat16
HIGHEST = lax.Precision.HIGHEST

NT = (((1,), (1,)), ((), ()))
NN = (((1,), (0,)), ((), ()))
TN = (((0,), (0,)), ((), ()))

SIDE = 4
CORES = 2
BLK = 256
VMEM = pl.BlockSpec(memory_space=pltpu.VMEM)
SMEM = pl.BlockSpec(memory_space=pltpu.SMEM)
HBM = pl.BlockSpec(memory_space=pltpu.HBM)


def params(mib):
    return pltpu.CompilerParams(vmem_limit_bytes=mib << 20)


def in_hbm(values):
    return [pltpu.with_memory_space_constraint(v, pltpu.HBM) for v in values]


def place():
    dp = lax.axis_index("dp").astype(jnp.int32)
    tensor = lax.axis_index("tensor").astype(jnp.int32)
    return lax.div(dp, SIDE), lax.rem(dp, SIDE), dp, lax.div(tensor, CORES), lax.rem(tensor, CORES)


def fetch(sources, targets, sems):
    copies = [pltpu.make_async_copy(a, b, sems.at[i]) for i, (a, b) in enumerate(zip(sources, targets))]
    for copy in copies:
        copy.start()
    return copies


def cost(flops, nbytes):
    return pl.CostEstimate(flops=flops, bytes_accessed=nbytes, transcendentals=0)


def split(value):
    high = value.astype(BF16)
    return high, (value - high.astype(F32)).astype(BF16)


def mm(a, b, dims):
    return lax.dot_general(a, b, dims, preferred_element_type=F32)


def mm3(a, b, dims):
    return mm(a[0], b[0], dims) + mm(a[1], b[0], dims) + mm(a[0], b[1], dims)


def along_z(step):
    return [(i, (i // SIDE) * SIDE + (i + step) % SIDE) for i in range(16)]


def along_x(step):
    return [(i, (i + step * SIDE) % 16) for i in range(16)]


def along_y(step):
    return [(i, (i + step * CORES) % 8) for i in range(8)]


def other_core():
    return [(i, i ^ 1) for i in range(8)]


def crossed(step, flip):
    pairs = []
    for dp in range(16):
        for tensor in range(8):
            table = along_x(step) if (tensor % CORES) ^ flip else along_z(step)
            pairs.append((dp * 8 + tensor, table[dp][1] * 8 + tensor))
    return pairs


def project_kernel(order, idx_in, idx_out, act, grad, bank_in, bank_out, out, proj_in, proj_out):
    @pl.when(pl.program_id(0) == 0)
    def _():
        for b in range(proj_in.shape[1] // 128):
            proj_in[:, b * 128 : (b + 1) * 128] = bank_in[idx_in[b]]
        for b in range(proj_out.shape[1] // 128):
            proj_out[:, b * 128 : (b + 1) * 128] = bank_out[idx_out[b]]

    out[0, :, 0:64] = mm(act[0], proj_in[...], NT)
    out[0, :, 64:128] = mm(grad[0], proj_out[...], NT)


def project(order, idx_in, idx_out, act, grad, bank_in_t, bank_out_t):
    idx_in, idx_out, act, grad, bank_in_t, bank_out_t = in_hbm(
        [idx_in, idx_out, act, grad, bank_in_t, bank_out_t]
    )
    count = order.shape[0]
    slots, width, model = act.shape[1], act.shape[2], grad.shape[2]
    return pl.pallas_call(
        project_kernel,
        out_shape=jax.ShapeDtypeStruct((count, slots, 128), F32),
        grid_spec=pltpu.PrefetchScalarGridSpec(
            num_scalar_prefetch=3,
            grid=(count,),
            in_specs=[
                pl.BlockSpec((1, slots, width), lambda i, o, a, b: (o[i], 0, 0)),
                pl.BlockSpec((1, slots, model), lambda i, o, a, b: (o[i], 0, 0)),
                pl.BlockSpec(bank_in_t.shape, lambda i, o, a, b: (0, 0, 0)),
                pl.BlockSpec(bank_out_t.shape, lambda i, o, a, b: (0, 0, 0)),
            ],
            out_specs=pl.BlockSpec((1, slots, 128), lambda i, o, a, b: (i, 0, 0)),
            scratch_shapes=[pltpu.VMEM((64, width), BF16), pltpu.VMEM((64, model), BF16)],
        ),
        compiler_params=params(12),
        cost_estimate=cost(2 * count * slots * (width + model) * 256, count * slots * (width + model) * 2),
        name="project",
    )(order, idx_in, idx_out, act, grad, bank_in_t, bank_out_t)


def factor_kernel(lens, a0, a1, b1, b2, b3, out, v0, v1, w1, w2, w3, sems):
    copies = fetch((a0, a1, b1, b2, b3), (v0, v1, w1, w2, w3), sems)
    _, _, _, y, core = place()
    for copy in copies:
        copy.wait()
    slots = v0.shape[1]
    for r in range(2):
        total = (v0[r] + v1[r]) + (w1[r] + w2[r]) + w3[r]
        used = lax.broadcasted_iota(jnp.int32, (slots, 64), 0) < lens[core * 8 + y * 2 + r]
        grad = jnp.where(used, total[:, 64:128], 0.0)
        out[r] = mm3(split(grad), split(total[:, 0:64]), TN)


def factor(lens, pieces):
    shape = pieces[0].shape
    return pl.pallas_call(
        factor_kernel,
        out_shape=jax.ShapeDtypeStruct((2, 64, 64), F32),
        in_specs=[SMEM] + [HBM] * 5,
        out_specs=VMEM,
        scratch_shapes=[pltpu.VMEM(shape, F32)] * 5 + [pltpu.SemaphoreType.DMA((5,))],
        name="factor",
    )(lens, *in_hbm(pieces))


def block_at(where, first, second):
    core = where[4]
    dx = core * first + (1 - core) * second
    dz = first + second - dx
    x = lax.rem(where[0] + SIDE - dx, SIDE)
    z = lax.rem(where[1] + SIDE - dz, SIDE)
    return pl.multiple_of((x * SIDE + z) * BLK, BLK)


def prior_kernel(g0, g1, g2, g3, prior_hbm, full_out, stack_out, pri_hi, pri_lo, out, g, prior, full, stack, sems):
    pieces = fetch((g0, g1, g2, g3), [g.at[i] for i in range(4)], sems)
    rows = [pl.ds(i * 64, 64) for i in range(4)]
    priors = fetch([prior_hbm.at[r] for r in rows], [prior.at[r] for r in rows], sems.at[pl.ds(4, 4)])
    where = place()
    for second in range(SIDE):
        pieces[second].wait()
        for first in range(SIDE):
            value = g[second, :, first * BLK : (first + 1) * BLK]
            at = pl.ds(block_at(where, first, second), BLK)
            full[:, at] = value
            stack[0:64, at], stack[64:128, at] = split(value)
    full_out[...] = full[...]
    stack_out[...] = stack[...]
    for i in range(4):
        priors[i].wait()
        for k in range(16):
            part = (rows[i], slice(k * BLK, (k + 1) * BLK))
            pri_hi[part], pri_lo[part] = split(prior[part])
    out[0:64, :] = local_image(stack, pri_hi, pri_lo)
    own = prior[:, pl.ds(pl.multiple_of(where[2] * BLK, BLK), BLK)]
    row = lax.broadcasted_iota(jnp.int32, (BLK, BLK), 0)
    col = lax.broadcasted_iota(jnp.int32, (BLK, BLK), 1)
    out[64:72, :] = jnp.broadcast_to(jnp.sum(jnp.where(row == col, own, 0.0), axis=0, keepdims=True), (8, BLK))


def prior_image(pieces, prior):
    n = prior.shape[1]
    sds = jax.ShapeDtypeStruct
    return pl.pallas_call(
        prior_kernel,
        out_shape=(
            pltpu.HBM((64, n), F32), pltpu.HBM((128, n), BF16), pltpu.HBM((BLK, n), BF16),
            pltpu.HBM((BLK, n), BF16), sds((72, BLK), F32),
        ),
        in_specs=[HBM] * 5,
        out_specs=(VMEM,) * 5,
        scratch_shapes=[
            pltpu.VMEM((4, 64, 4 * BLK), F32), pltpu.VMEM((BLK, n), F32),
            pltpu.VMEM((64, n), F32), pltpu.VMEM((128, n), BF16), pltpu.SemaphoreType.DMA((8,)),
        ],
        compiler_params=params(24),
        cost_estimate=cost(6 * 256 * 256 * n, 8 * 256 * n),
        name="prior_image",
    )(*in_hbm([*pieces, prior]))


def rowsum(value):
    return jnp.sum(value, axis=1, keepdims=True)


def local_image(stack, cov_hi, cov_lo):
    both = mm(stack[...], cov_hi[...], NT)
    return both[0:64] + both[64:128] + mm(stack[0:64, :], cov_lo[...], NT)


def next_direction(res, direc, stack, beta, old):
    for k in range(16):
        cols = slice(k * BLK, (k + 1) * BLK)
        value = res[:, cols] + beta * old[:, cols]
        direc[:, cols] = value
        high, low = split(value)
        stack[0:64, cols] = high
        stack[64:128, cols] = low


def own_scores(stack, own_hi, own_lo):
    both = mm(stack[...], own_hi[...], NT)
    return both[0:64] + both[64:128] + mm(stack[0:64, :], own_lo[...], NT)


def first_kernel(
    n0, n1, n2, n3, m0, m1, m2, m3, start_hbm, stack_hbm, image_hbm, pri_hi_hbm, pri_lo_hbm,
    res, direc, rr, score, query, damp, out, f_hi, f_lo, own_hi, own_lo,
    pieces, start, start_stack, image, pri_hi, pri_lo, stack, sems,
):
    begin = fetch((stack_hbm, start_hbm), (start_stack, start), sems)
    copies = fetch((n0, n1, n2, n3, m0, m1, m2, m3), [pieces.at[i] for i in range(8)], sems.at[pl.ds(5, 8)])
    later = fetch((image_hbm, pri_hi_hbm, pri_lo_hbm), (image, pri_hi, pri_lo), sems.at[pl.ds(2, 3)])
    where = place()
    square = jnp.zeros((32, BLK), F32)
    for i in range(8):
        copies[i].wait()
        rows = slice(i * 32, (i + 1) * 32)
        for k in range(16):
            cols = slice(k * BLK, (k + 1) * BLK)
            value = pieces[i, :, cols]
            square = square + value * value
            f_hi[rows, cols], f_lo[rows, cols] = split(value)
    for copy in begin:
        copy.wait()
    rollouts = f_hi.shape[0]
    half = rollouts // 2
    for ref, f in ((own_hi, f_hi), (own_lo, f_lo)):
        ref[0:8, :] = f[0:8, :]
        ref[8:16, :] = f[half : half + 8, :]

    q = local_image(start_stack, f_hi, f_lo)
    later[0].wait()
    diag = jnp.zeros((8, BLK), F32)
    for i in range(16):
        diag = diag + image[i, 64:72, :]
    features = f_hi.shape[1]
    trace = jnp.sum(diag) / 8.0 + jnp.sum(square) / rollouts
    damping = 0.1 * trace / features
    damp[...] = jnp.full(damp.shape, damping, F32)
    q_parts = split(q * (1.0 / rollouts))
    norm = jnp.zeros((64, 1), F32)
    curve = jnp.zeros((64, 1), F32)
    for k in range(16):
        cols = slice(k * BLK, (k + 1) * BLK)
        b = start[:, cols]
        value = image[k, 0:64, :] + mm3(q_parts, (f_hi[:, cols], f_lo[:, cols]), NN) + damping * b
        res[:, cols] = value
        norm = norm + rowsum(b * b)
        curve = curve + rowsum(b * value)
    alpha = norm / curve
    fresh = jnp.zeros((64, 1), F32)
    for k in range(16):
        cols = slice(k * BLK, (k + 1) * BLK)
        value = start[:, cols] - alpha * res[:, cols]
        res[:, cols] = value
        fresh = fresh + rowsum(value * value)
    next_direction(res, direc, stack, fresh / norm, start)
    rr[...] = jnp.broadcast_to(fresh, rr.shape)
    score[:, 0:8] = alpha * q[:, 0:8]
    score[:, 8:16] = alpha * q[:, half : half + 8]

    mine = pl.ds(pl.multiple_of(where[2] * BLK, BLK), BLK)
    q = local_image(stack, f_hi, f_lo)
    query[:, 0:8] = q[:, 0:8]
    query[:, 8:16] = q[:, half : half + 8]
    low_rank = mm3(split(q * (1.0 / rollouts)), (f_hi[:, mine], f_lo[:, mine]), NN)
    later[1].wait()
    later[2].wait()
    out[...] = local_image(stack, pri_hi, pri_lo) + low_rank + damping * direc[:, mine]


def first_step(pieces, start, start_stack, image, prior):
    n = start.shape[1]
    sds = jax.ShapeDtypeStruct
    return pl.pallas_call(
        first_kernel,
        out_shape=(
            sds((64, n), F32), sds((64, n), F32), sds((64, 128), F32),
            sds((64, 16), F32), sds((64, 16), F32), sds((8, 128), F32), sds((64, BLK), F32),
            sds((256, n), BF16), sds((256, n), BF16), sds((16, n), BF16), sds((16, n), BF16),
        ),
        in_specs=[HBM] * 13,
        out_specs=(VMEM,) * 11,
        scratch_shapes=[
            pltpu.VMEM((8, 32, n), F32), pltpu.VMEM((64, n), F32), pltpu.VMEM((128, n), BF16),
            pltpu.VMEM(image.shape, F32), pltpu.VMEM((BLK, n), BF16), pltpu.VMEM((BLK, n), BF16),
            pltpu.VMEM((128, n), BF16), pltpu.SemaphoreType.DMA((13,)),
        ],
        compiler_params=params(32),
        name="first_step",
    )(*in_hbm([*pieces, start, start_stack, image, *prior]))


def covariance_kernel(f_hi, f_lo, prior, damp, cov_hi, cov_lo):
    first = pl.multiple_of(place()[2] * BLK, BLK)
    mine = (f_hi[:, pl.ds(first, BLK)], f_lo[:, pl.ds(first, BLK)])
    row = lax.broadcasted_iota(jnp.int32, (BLK, BLK), 0)
    col = lax.broadcasted_iota(jnp.int32, (BLK, BLK), 1)
    for k in range(16):
        cols = slice(k * BLK, (k + 1) * BLK)
        value = prior[:, cols] + mm3(mine, (f_hi[:, cols], f_lo[:, cols]), TN) * (1.0 / f_hi.shape[0])
        value = value + jnp.where(row + first == col + k * BLK, damp[0:1, 0:1], 0.0)
        cov_hi[:, cols], cov_lo[:, cols] = split(value)


def covariance(f_hi, f_lo, prior, damp):
    n = prior.shape[1]
    return pl.pallas_call(
        covariance_kernel,
        out_shape=(jax.ShapeDtypeStruct((BLK, n), BF16),) * 2,
        in_specs=[VMEM] * 4,
        out_specs=(VMEM, VMEM),
        compiler_params=params(20),
        cost_estimate=cost(6 * 256 * 256 * n, 12 * 256 * n),
        name="covariance",
    )(f_hi, f_lo, prior, damp)


def step_kernel(
    g0, g1, g2, g3, res_in, direc_in, rr_in, score_in, query_in, cov_hi, cov_lo, own_hi, own_lo,
    rr, score, query, out, res, direc, stack, *, last,
):
    where = place()
    curve = jnp.zeros((64, 1), F32)
    for second, piece in enumerate((g0, g1, g2, g3)):
        for first in range(SIDE):
            at = pl.ds(block_at(where, first, second), BLK)
            curve = curve + rowsum(direc_in[:, at] * piece[:, first * BLK : (first + 1) * BLK])
    norm = rr_in[:, 0:1]
    alpha = norm / curve
    fresh = jnp.zeros((64, 1), F32)
    for second, piece in enumerate((g0, g1, g2, g3)):
        for first in range(SIDE):
            at = pl.ds(block_at(where, first, second), BLK)
            value = res_in[:, at] - alpha * piece[:, first * BLK : (first + 1) * BLK]
            res[:, at] = value
            fresh = fresh + rowsum(value * value)
    next_direction(res, direc, stack, fresh / norm, direc_in)
    rr[...] = jnp.broadcast_to(fresh, rr.shape)
    score[...] = score_in[...] + alpha * query_in[...]
    image = local_image(stack, cov_hi, cov_lo)
    query[...] = own_scores(stack, own_hi, own_lo)
    if last:
        mine = direc[:, pl.ds(pl.multiple_of(where[2] * BLK, BLK), BLK)]
        ones = jnp.ones((8, BLK), F32)
        curve = lax.dot_general(ones, mine * image, NT, precision=HIGHEST, preferred_element_type=F32)
        for i in range(16):
            out[i, :, 0:64] = curve
            out[i, :, 64:128] = curve
    else:
        out[...] = image


def cg_step(pieces, state, cov, last):
    n = cov[0].shape[1]
    sds = jax.ShapeDtypeStruct
    small = (
        sds((64, 128), F32), sds((64, 16), F32), sds((64, 16), F32),
        sds((16, 8, 128) if last else (64, BLK), F32),
    )
    large = [] if last else [sds((64, n), F32)] * 2
    scratch = [pltpu.VMEM((64, n), F32)] * 2 if last else []
    return pl.pallas_call(
        functools.partial(step_kernel, last=last),
        out_shape=(*small, *large),
        in_specs=[VMEM] * 13,
        out_specs=(VMEM,) * (4 + len(large)),
        scratch_shapes=[*scratch, pltpu.VMEM((128, n), BF16)],
        compiler_params=params(20),
        name="last_step" if last else "cg_step",
    )(*pieces, *state, *cov)


def finish_kernel(sums, rr, score, query, out):
    curve = sums[0]
    for i in range(1, 16):
        curve = curve + sums[i]
    dot = functools.partial(lax.dot_general, dimension_numbers=NT, precision=HIGHEST, preferred_element_type=F32)
    eye = lax.broadcasted_iota(jnp.int32, (64, 64), 0) == lax.broadcasted_iota(jnp.int32, (64, 64), 1)
    norm = jnp.sum(jnp.where(eye, jnp.broadcast_to(rr[:, 0:1], (64, 64)), 0.0), axis=0, keepdims=True)
    alpha = norm / curve[0:1, 0:64]
    _, _, _, y_here, core_here = place()
    row = lax.broadcasted_iota(jnp.int32, (16, 16), 0)
    slot = lax.broadcasted_iota(jnp.int32, (16, 16), 1)
    core = lax.rem(slot // 8 + core_here, CORES)
    y = lax.rem(y_here + SIDE - lax.rem(slot, 8) // 2, SIDE)
    pick = (row == core * 8 + y * 2 + lax.rem(slot, 2)).astype(F32)
    out[...] = dot(pick, score[...]) + alpha * dot(pick, query[...])


def finish(sums, rr, score, query):
    return pl.pallas_call(
        finish_kernel,
        out_shape=jax.ShapeDtypeStruct((16, 64), F32),
        in_specs=[VMEM] * 4,
        out_specs=VMEM,
        name="finish",
    )(sums, rr, score, query)


BOTH = ("dp", "tensor")


def first_stage(block):
    line = [block] + [lax.ppermute(block, BOTH, crossed(d, 0)) for d in (1, 2, 3)]
    return jnp.concatenate(line, axis=1)


def second_stage(line):
    return [line] + [lax.ppermute(line, BOTH, crossed(d, 1)) for d in (1, 2, 3)]


def per_device(
    activations, out_grads, lengths, bank_in, index_in, bank_out, index_out, prior_cov, val_grads
):
    _, _, _, y, core = place()
    slot = jnp.arange(8, dtype=jnp.int32)
    line = lax.rem(y + slot // 2, SIDE) * 2 + slot % 2

    banks = (bank_in.transpose(0, 2, 1), bank_out.transpose(0, 2, 1))
    start_line = first_stage(val_grads.T)
    theirs = project((1 - core) * 8 + line, index_in, index_out, activations, out_grads, *banks)
    order, start_line, theirs = lax.optimization_barrier((core * 8 + line, start_line, theirs))
    start_pieces = second_stage(start_line)
    from_core = lax.ppermute(theirs, "tensor", other_core())
    mine = project(order, index_in, index_out, activations, out_grads, *banks)
    mine, start_pieces = lax.optimization_barrier((mine, start_pieces))
    from_y = [
        lax.ppermute(mine[2 * d : 2 * d + 2] + from_core[2 * d : 2 * d + 2], "tensor", along_y(d))
        for d in (1, 2, 3)
    ]

    start, start_stack, pri_hi, pri_lo, image_here = prior_image(start_pieces, prior_cov)
    image = lax.all_gather(image_here, "dp", axis=0)
    lengths, start = lax.optimization_barrier((lengths, start))

    own = factor(lengths, [mine[0:2], from_core[0:2], *from_y]).reshape(2, 4096)
    part = jnp.concatenate([own] + [lax.ppermute(own, "tensor", along_y(d)) for d in (1, 2, 3)], axis=0)
    moved = [lax.ppermute(part, BOTH, crossed(d, 0)) for d in (1, 2, 3)]
    near = second_stage(jnp.concatenate([part] + moved, axis=0))
    far = [lax.ppermute(piece, "tensor", other_core()) for piece in near]

    first = first_step(near + far, start, start_stack, image, (pri_hi, pri_lo))
    state, damp, out, f_hi, f_lo, own_hi, own_lo = first[0:5], *first[5:11]
    cov = (*covariance(f_hi, f_lo, prior_cov, damp), own_hi, own_lo)
    for iteration in range(1, ITERS - 1):
        pieces = second_stage(first_stage(out))
        rr, score, query, out, *large = cg_step(pieces, state, cov, iteration + 2 == ITERS)
        state = (*large, rr, score, query)
    sums = lax.all_to_all(out, "dp", 0, 0, tiled=True)
    return finish(sums, rr, score, query)


def solution(mesh):
    return jax.shard_map(
        per_device,
        mesh=mesh,
        in_specs=(
            P("dp", None, "tensor"),
            P("dp", None, "tensor"),
            P("dp"),
            P(),
            P("tensor"),
            P(),
            P("tensor"),
            P("dp", None),
            P("dp", "tensor"),
        ),
        out_specs=P("dp", "tensor"),
        check_vma=False,
    )
```

time: 292 us -> 230 us (0.79)
  local copies, waits for them, and re-layouts: 35.2 us -> 3.26 us
  starting transfers between devices: 69 us -> 45.9 us
  waiting for transfers between devices: 110 us -> 102 us
  Pallas kernels: 47.9 us -> 52.4 us
    all_gather x1, waiting for transfers between devices: 33.7 us -> 0.02 us  [per_device(): image = lax.all_gather(image_here, 'dp', axis=0)]
    unnamed x58 -> x48, local copies, waits for them, and re-layouts: 24.3 us -> 2.18 us
    ppermute x37 -> x40, starting transfers between devices: 57.8 us -> 39 us  [the longest x18 18.3 us: second_stage(): return [line] + [lax.ppermute(line, BOTH, crossed(d, 1)) for d in (1, 2, 3)]]
    ppermute x37 -> x40, waiting for transfers between devices: 66 us -> 84.2 us  [the longest x18 50.6 us: second_stage(): return [line] + [lax.ppermute(line, BOTH, crossed(d, 1)) for d in (1, 2, 3)]]
    concatenate x6 -> x5, local copies, waits for them, and re-layouts: 8.19 us -> 0.16 us  [the longest x1 0.13 us: per_device(): near = second_stage(jnp.concatenate([part] + moved, axis=0))]
    pallas_call x2, Pallas kernels: 9.68 us -> 17.7 us  [project(): pl.pallas_call(project_kernel, out_shape=jax.ShapeDtypeStruct((count, slo...]
    ppermute x3, waiting for transfers between devices: 0.01 us -> 4.55 us  [per_device(): lax.ppermute(own, 'tensor', along_y(d))]
    pallas_call x5 -> x6, Pallas kernels: 22.3 us -> 18 us  [the longest x4 9.87 us: cg_step(): pl.pallas_call(functools.partial(step_kernel, last=last), out_shape=(*sma...]
  transfers between devices with their start and end apart: 45 -> 48, of which waited for: 28 -> 28; matrix products, arithmetic and copies ran while one was open for 3% -> 1% of each run, Pallas kernels for 3% -> 13%
where the time goes in v2:
time: 230 us; the launch traced here: 229 us
  waiting for transfers between devices  102 us (44%)
  Pallas kernels  52.4 us (23%)
  starting transfers between devices  45.9 us (20%)
  between operations  13.9 us (6%)
  blocking collectives  10.9 us (5%)
  local copies, waits for them, and re-layouts  3.26 us (1%)
    ppermute x18, waiting for transfers between devices, second_stage(): return [line] + [lax.ppermute(line, BOTH, crossed(d, 1)) for d in (1, 2, 3)]  50.6 us
    ppermute x15, waiting for transfers between devices, first_stage(): lax.ppermute(block, BOTH, crossed(d, 0))  23.2 us
    ppermute x18, starting transfers between devices, second_stage(): return [line] + [lax.ppermute(line, BOTH, crossed(d, 1)) for d in (1, 2, 3)]  18.3 us
    pallas_call x2, Pallas kernels, project(): pl.pallas_call(project_kernel, out_shape=jax.ShapeDtypeStruct((count, slo...  17.7 us
    ppermute x15, starting transfers between devices, first_stage(): lax.ppermute(block, BOTH, crossed(d, 0))  16.2 us
    ppermute x3, waiting for transfers between devices, per_device(): lax.ppermute(mine[2 * d:2 * d + 2] + from_core[2 * d:2 * d + 2], 'tensor'...  13.2 us
    pallas_call x1, Pallas kernels, first_step(): pl.pallas_call(first_kernel, out_shape=(sds((64, n), F32), sds((64, n), F...  12.1 us
    all_to_all x1, blocking collectives, per_device(): sums = lax.all_to_all(out, 'dp', 0, 0, tiled=True)  10.9 us
  transfers between devices with their start and end apart: 48, of which 28 were waited for; matrix products, arithmetic and copies ran while one was open for 1% of the time, Pallas kernels for 13%

profile of v2, /device:TPU:0, one launch (start us, length us, event | category | flops | bytes accessed | tf_op | source)
XLA Modules:
  0.0 229.3 jit_solution(12936344605906938981)
XLA Ops:
  6.5 4.1 %collective-permute-start.2 = (f32[64,256]{1,0:T(8,128)}, f32[64,256]{1,0:T(8,128)S(1)}, u32[]{:S(2)}, u32[]{:S(2)}) collective-permute-start(f32[64,256]{1,0:T(8,128)} %bitcast.9), channel_id=1, source_target_pairs={{0,24},{1,97},{2,26},{3,99},{4,28},{5,101},{6,30},{7,103},{8,0},{9... | collective-permute-start | bytes 196616 | tf_op jit(solution)/shard_map/ppermute | solution.py:434
  11.9 8.9 %project.2 = f32[8,256,128]{2,1,0:T(8,128)S(1)} custom-call(s32[8]{0:T(128)S(1)} %get-tuple-element.110.order, s32[14]{0:T(128)} %idx_in.3, s32[4]{0:T(128)} %idx_out.3, bf16[16,256,1792]{2,1,0:T(8,128)(2,1)} %act.3, bf16[16,256,512]{2,1,0:T(8,128)(2,1)} %grad.3, bf16[16,64,128]{2,1,0:T(8,128)(2,1)} %bitcast.5, bf16[16,64,128]{2,1,0:T(8,128)(2,1)} %bitcast.7), custom_call_target="tpu_custom_call" | custom-call | flops 2415919104 | bytes 9437184 | tf_op jit(solution)/shard_map/project/pallas_call | solution.py:108
  21.0 2.8 %collective-permute-start.5 = (f32[64,1024]{1,0:T(8,128)S(1)}, f32[64,1024]{1,0:T(8,128)S(1)}, u32[]{:S(2)}, u32[]{:S(2)}) collective-permute-start(f32[64,1024]{1,0:T(8,128)S(1)} %pad_maximum_fusion.g0), channel_id=1, source_target_pairs={{0,96},{1,25},{2,98},{3,27},{4,100},{5,29},{6,102},{7,31},{8,104},... | collective-permute-start | bytes 786440 | tf_op jit(solution)/shard_map/ppermute | solution.py:439
  25.5 8.8 %project.3 = f32[8,256,128]{2,1,0:T(8,128)S(1)} custom-call(s32[8]{0:T(128)S(1)} %get-tuple-element.55.order, s32[14]{0:T(128)} %idx_in.3, s32[4]{0:T(128)} %idx_out.3, bf16[16,256,1792]{2,1,0:T(8,128)(2,1)} %act.3, bf16[16,256,512]{2,1,0:T(8,128)(2,1)} %grad.3, bf16[16,64,128]{2,1,0:T(8,128)(2,1)} %bitcast.6, bf16[16,64,128]{2,1,0:T(8,128)(2,1)} %bitcast.8), custom_call_target="tpu_custom_call" | custom-call | flops 2415919104 | bytes 9437184 | tf_op jit(solution)/shard_map/project/pallas_call | solution.py:108
  35.8 5.7 %prior_image.1 = (f32[64,4096]{1,0:T(8,128)}, bf16[128,4096]{1,0:T(8,128)(2,1)}, bf16[256,4096]{1,0:T(8,128)(2,1)}, bf16[256,4096]{1,0:T(8,128)(2,1)}, f32[72,256]{1,0:T(8,128)}) custom-call(f32[64,1024]{1,0:T(8,128)} %copy-done.13, f32[64,1024]{1,0:T(8,128)} %copy-done.17, f32[64,1024]{1,0:T(8,128)} %copy-done.16, f32[64,1024]{1,0:T(8,128)} %copy-done.15, ...), custom_call_target="tpu_custom_call" | custom-call | flops 1610612736 | bytes 8388608 | tf_op jit(solution)/shard_map/prior_image/pallas_call | solution.py:192
  42.5 3.0 %collective-permute-start.9 = (f32[2,256,128]{2,1,0:T(8,128)S(1)}, f32[2,256,128]{2,1,0:T(8,128)S(1)}, u32[]{:S(2)}, u32[]{:S(2)}) collective-permute-start(f32[2,256,128]{2,1,0:T(8,128)S(1)} %get-tuple-element.105), channel_id=1, source_target_pairs={{0,6},{1,7},{2,0},{3,1},{4,2},{5,3},{6,4},{7,5},{8,14},{9,15},{10,... | collective-permute-start | bytes 786440 | tf_op jit(solution)/shard_map/ppermute | solution.py:458
  47.1 9.5 %collective-permute-done.9.b3 = f32[2,256,128]{2,1,0:T(8,128)S(1)} collective-permute-done((f32[2,256,128]{2,1,0:T(8,128)S(1)}, f32[2,256,128]{2,1,0:T(8,128)S(1)}, u32[]{:S(2)}, u32[]{:S(2)}) %collective-permute-start.9) | collective-permute-done | bytes 262176 | tf_op jit(solution)/shard_map/ppermute | solution.py:458
  56.6 3.7 %collective-permute-done.7.b1 = f32[2,256,128]{2,1,0:T(8,128)S(1)} collective-permute-done((f32[2,256,128]{2,1,0:T(8,128)S(1)}, f32[2,256,128]{2,1,0:T(8,128)S(1)}, u32[]{:S(2)}, u32[]{:S(2)}) %collective-permute-start.7) | collective-permute-done | bytes 262176 | tf_op jit(solution)/shard_map/ppermute | solution.py:458
  61.0 3.0 %factor.1 = f32[2,64,64]{2,1,0:T(8,128)} custom-call(s32[16]{0:T(128)} %lens, f32[2,256,128]{2,1,0:T(8,128)} %get-tuple-element.108.a0, f32[2,256,128]{2,1,0:T(8,128)} %get-tuple-element.109.a1, f32[2,256,128]{2,1,0:T(8,128)} %copy-done.12, f32[2,256,128]{2,1,0:T(8,128)} %copy-done.11, f32[2,256,128]{2,1,0:T(8,128)} %copy-done.10), custom_call_target="tpu_custom_call" | custom-call | tf_op jit(solution)/shard_map/factor/pallas_call | solution.py:144
  71.7 3.0 %collective-permute-start.15 = (f32[8,4096]{1,0:T(8,128)S(1)}, f32[8,4096]{1,0:T(8,128)S(1)}, u32[]{:S(2)}, u32[]{:S(2)}) collective-permute-start(f32[8,4096]{1,0:T(8,128)S(1)} %pad_maximum_fusion.1), channel_id=1, source_target_pairs={{0,24},{1,97},{2,26},{3,99},{4,28},{5,101},{6,30},{7,103},{8,0},{9... | collective-permute-start | bytes 393224 | tf_op jit(solution)/shard_map/ppermute | solution.py:468
  75.6 4.7 %collective-permute-done.15 = f32[8,4096]{1,0:T(8,128)S(1)} collective-permute-done((f32[8,4096]{1,0:T(8,128)S(1)}, f32[8,4096]{1,0:T(8,128)S(1)}, u32[]{:S(2)}, u32[]{:S(2)}) %collective-permute-start.15) | collective-permute-done | bytes 131104 | tf_op jit(solution)/shard_map/ppermute | solution.py:468
  88.1 10.4 %collective-permute-done.18.n3 = f32[32,4096]{1,0:T(8,128)S(1)} collective-permute-done((f32[32,4096]{1,0:T(8,128)S(1)}, f32[32,4096]{1,0:T(8,128)S(1)}, u32[]{:S(2)}, u32[]{:S(2)}) %collective-permute-start.18) | collective-permute-done | bytes 524320 | tf_op jit(solution)/shard_map/ppermute | solution.py:439
  99.1 3.4 %collective-permute-done.16.n1 = f32[32,4096]{1,0:T(8,128)S(1)} collective-permute-done((f32[32,4096]{1,0:T(8,128)S(1)}, f32[32,4096]{1,0:T(8,128)S(1)}, u32[]{:S(2)}, u32[]{:S(2)}) %collective-permute-start.16) | collective-permute-done | bytes 524320 | tf_op jit(solution)/shard_map/ppermute | solution.py:439
  104.6 12.1 %first_step.1 = (f32[64,4096]{1,0:T(8,128)S(1)}, f32[64,4096]{1,0:T(8,128)S(1)}, f32[64,128]{1,0:T(8,128)S(1)}, f32[64,16]{1,0:T(8,128)S(1)}, f32[64,16]{1,0:T(8...) custom-call(f32[32,4096]{1,0:T(8,128)} %copy-done.4, ...), custom_call_target="tpu_custom_call" | custom-call | tf_op jit(solution)/shard_map/first_step/pallas_call | solution.py:304
  119.4 5.5 %collective-permute-done.23 = f32[64,256]{1,0:T(8,128)S(1)} collective-permute-done((f32[64,256]{1,0:T(8,128)S(1)}, f32[64,256]{1,0:T(8,128)S(1)}, u32[]{:S(2)}, u32[]{:S(2)}) %collective-permute-start.23) | collective-permute-done | bytes 65568 | tf_op jit(solution)/shard_map/ppermute | solution.py:434
  127.5 2.5 %covariance.1 = (bf16[256,4096]{1,0:T(8,128)(2,1)S(1)}, bf16[256,4096]{1,0:T(8,128)(2,1)S(1)}) custom-call(bf16[256,4096]{1,0:T(8,128)(2,1)S(1)} %get-tuple-element.76.f_hi, bf16[256,4096]{1,0:T(8,128)(2,1)S(1)} %get-tuple-element.77.f_lo, f32[256,4096]{1,0:T(8,128)S(1)} %copy-done, f32[8,128]{1,0:T(8,128)S(1)} %get-tuple-element.78.damp), custom_call_target="tpu_custom_call" | custom-call | flops 1610612736 | bytes 12582912 | tf_op jit(solution)/shard_map/covariance/pallas_call | solution.py:337
  131.3 2.8 %collective-permute-done.27.g2 = f32[64,1024]{1,0:T(8,128)S(1)} collective-permute-done((f32[64,1024]{1,0:T(8,128)S(1)}, f32[64,1024]{1,0:T(8,128)S(1)}, u32[]{:S(2)}, u32[]{:S(2)}) %collective-permute-start.27) | collective-permute-done | bytes 262176 | tf_op jit(solution)/shard_map/ppermute | solution.py:439
  134.2 2.7 %collective-permute-done.26.g1 = f32[64,1024]{1,0:T(8,128)S(1)} collective-permute-done((f32[64,1024]{1,0:T(8,128)S(1)}, f32[64,1024]{1,0:T(8,128)S(1)}, u32[]{:S(2)}, u32[]{:S(2)}) %collective-permute-start.26) | collective-permute-done | bytes 262176 | tf_op jit(solution)/shard_map/ppermute | solution.py:439
  136.9 2.4 %cg_step.3 = (f32[64,128]{1,0:T(8,128)S(1)}, f32[64,16]{1,0:T(8,128)S(1)}, f32[64,16]{1,0:T(8,128)S(1)}, f32[64,256]{1,0:T(8,128)S(1)}, f32[64,4096]{1,0:T(8,128)S(1)}, /*index=5*/f32[64,4096]{1,0:T(8,128)S(1)}) custom-call(f32[64,1024]{1,0:T(8,128)S(1)} %constant_dynamic-update-slice_fusion.g0, f32[64,1024]{1,0:T(8,128)S(1)} %collective-permute-done.26.g1, ...), custom_call_target="tpu_custom_call" | custom-call | tf_op jit(solution)/shard_map/cg_step/pallas_call | solution.py:392
  142.1 4.6 %collective-permute-done.29 = f32[64,256]{1,0:T(8,128)S(1)} collective-permute-done((f32[64,256]{1,0:T(8,128)S(1)}, f32[64,256]{1,0:T(8,128)S(1)}, u32[]{:S(2)}, u32[]{:S(2)}) %collective-permute-start.29) | collective-permute-done | bytes 65568 | tf_op jit(solution)/shard_map/ppermute | solution.py:434
  149.1 4.0 %collective-permute-done.34.g3 = f32[64,1024]{1,0:T(8,128)S(1)} collective-permute-done((f32[64,1024]{1,0:T(8,128)S(1)}, f32[64,1024]{1,0:T(8,128)S(1)}, u32[]{:S(2)}, u32[]{:S(2)}) %collective-permute-start.34) | collective-permute-done | bytes 262176 | tf_op jit(solution)/shard_map/ppermute | solution.py:439
  155.4 2.7 %collective-permute-done.32.g1 = f32[64,1024]{1,0:T(8,128)S(1)} collective-permute-done((f32[64,1024]{1,0:T(8,128)S(1)}, f32[64,1024]{1,0:T(8,128)S(1)}, u32[]{:S(2)}, u32[]{:S(2)}) %collective-permute-start.32) | collective-permute-done | bytes 262176 | tf_op jit(solution)/shard_map/ppermute | solution.py:439
  163.4 8.3 %collective-permute-done.35 = f32[64,256]{1,0:T(8,128)S(1)} collective-permute-done((f32[64,256]{1,0:T(8,128)S(1)}, f32[64,256]{1,0:T(8,128)S(1)}, u32[]{:S(2)}, u32[]{:S(2)}) %collective-permute-start.35) | collective-permute-done | bytes 65568 | tf_op jit(solution)/shard_map/ppermute | solution.py:434
  174.1 4.0 %collective-permute-done.40.g3 = f32[64,1024]{1,0:T(8,128)S(1)} collective-permute-done((f32[64,1024]{1,0:T(8,128)S(1)}, f32[64,1024]{1,0:T(8,128)S(1)}, u32[]{:S(2)}, u32[]{:S(2)}) %collective-permute-start.40) | collective-permute-done | bytes 262176 | tf_op jit(solution)/shard_map/ppermute | solution.py:439
  178.1 2.7 %collective-permute-done.39.g2 = f32[64,1024]{1,0:T(8,128)S(1)} collective-permute-done((f32[64,1024]{1,0:T(8,128)S(1)}, f32[64,1024]{1,0:T(8,128)S(1)}, u32[]{:S(2)}, u32[]{:S(2)}) %collective-permute-start.39) | collective-permute-done | bytes 262176 | tf_op jit(solution)/shard_map/ppermute | solution.py:439
  180.9 4.1 %collective-permute-done.38.g1 = f32[64,1024]{1,0:T(8,128)S(1)} collective-permute-done((f32[64,1024]{1,0:T(8,128)S(1)}, f32[64,1024]{1,0:T(8,128)S(1)}, u32[]{:S(2)}, u32[]{:S(2)}) %collective-permute-start.38) | collective-permute-done | bytes 262176 | tf_op jit(solution)/shard_map/ppermute | solution.py:439
  189.9 4.9 %collective-permute-done.41 = f32[64,256]{1,0:T(8,128)S(1)} collective-permute-done((f32[64,256]{1,0:T(8,128)S(1)}, f32[64,256]{1,0:T(8,128)S(1)}, u32[]{:S(2)}, u32[]{:S(2)}) %collective-permute-start.41) | collective-permute-done | bytes 65568 | tf_op jit(solution)/shard_map/ppermute | solution.py:434
  197.3 4.0 %collective-permute-done.46.g3 = f32[64,1024]{1,0:T(8,128)S(1)} collective-permute-done((f32[64,1024]{1,0:T(8,128)S(1)}, f32[64,1024]{1,0:T(8,128)S(1)}, u32[]{:S(2)}, u32[]{:S(2)}) %collective-permute-start.46) | collective-permute-done | bytes 262176 | tf_op jit(solution)/shard_map/ppermute | solution.py:439
  201.2 2.8 %collective-permute-done.45.g2 = f32[64,1024]{1,0:T(8,128)S(1)} collective-permute-done((f32[64,1024]{1,0:T(8,128)S(1)}, f32[64,1024]{1,0:T(8,128)S(1)}, u32[]{:S(2)}, u32[]{:S(2)}) %collective-permute-start.45) | collective-permute-done | bytes 262176 | tf_op jit(solution)/shard_map/ppermute | solution.py:439
  204.1 3.1 %collective-permute-done.44.g1 = f32[64,1024]{1,0:T(8,128)S(1)} collective-permute-done((f32[64,1024]{1,0:T(8,128)S(1)}, f32[64,1024]{1,0:T(8,128)S(1)}, u32[]{:S(2)}, u32[]{:S(2)}) %collective-permute-start.44) | collective-permute-done | bytes 262176 | tf_op jit(solution)/shard_map/ppermute | solution.py:439
  207.1 2.7 %last_step.1 = (f32[64,128]{1,0:T(8,128)S(1)}, f32[64,16]{1,0:T(8,128)S(1)}, f32[64,16]{1,0:T(8,128)S(1)}, f32[16,8,128]{2,1,0:T(8,128)S(1)}) custom-call(f32[64,1024]{1,0:T(8,128)S(1)} %constant_dynamic-update-slice_fusion.12.g0, f32[64,1024]{1,0:T(8,128)S(1)} %collective-permute-done.44.g1, f32[64,1024]{1,0:T(8,128)S(1)} %collective-permute-done.45.g2, ...), custom_call_target="tpu_custom_call" | custom-call | tf_op jit(solution)/shard_map/last_step/pallas_call | solution.py:392
  209.8 10.9 %all_to_all.5.sums = f32[16,8,128]{2,1,0:T(8,128)} all-to-all(f32[16,8,128]{2,1,0:T(8,128)S(1)} %get-tuple-element.101), channel_id=1, replica_groups=mesh['dp'=16,'tensor'=8] {'dp'}, dimensions={0} | all-to-all | bytes 131072 | tf_op jit(solution)/shard_map/all_to_all | solution.py:479
  (135 shorter events, 57.8 us)
Async XLA Ops:
  6.5 96.0 %all-gather.3.cloned.1.call-start = ((), (), s32[]{:S(2)}) async-start(), calls=%async_computation.1 | async-start | bytes 1253376 | tf_op jit(solution)/shard_map/all_gather | solution.py:463
  6.5 14.3 %collective-permute-start.2 = (f32[64,256]{1,0:T(8,128)}, f32[64,256]{1,0:T(8,128)S(1)}, u32[]{:S(2)}, u32[]{:S(2)}) collective-permute-start(f32[64,256]{1,0:T(8,128)} %bitcast.9), channel_id=1, source_target_pairs={{0,24},{1,97},{2,26},{3,99},{4,28},{5,101},{6,30},{7,103},{8,0},{9... | collective-permute-start | bytes 196616 | tf_op jit(solution)/shard_map/ppermute | solution.py:434
  10.7 10.2 %collective-permute-start.1 = (f32[64,256]{1,0:T(8,128)}, f32[64,256]{1,0:T(8,128)S(1)}, u32[]{:S(2)}, u32[]{:S(2)}) collective-permute-start(f32[64,256]{1,0:T(8,128)} %bitcast.10), channel_id=1, source_target_pairs={{0,16},{1,65},{2,18},{3,67},{4,20},{5,69},{6,22},{7,71},{8,24},{9,... | collective-permute-start | bytes 196616 | tf_op jit(solution)/shard_map/ppermute | solution.py:434
  10.7 10.2 %collective-permute-start = (f32[64,256]{1,0:T(8,128)}, f32[64,256]{1,0:T(8,128)S(1)}, u32[]{:S(2)}, u32[]{:S(2)}) collective-permute-start(f32[64,256]{1,0:T(8,128)} %bitcast.11), channel_id=1, source_target_pairs={{0,8},{1,33},{2,10},{3,35},{4,12},{5,37},{6,14},{7,39},{8,16},{9,4... | collective-permute-start | bytes 196616 | tf_op jit(solution)/shard_map/ppermute | solution.py:434
  20.9 20.6 %collective-permute-start.6 = (f32[8,256,128]{2,1,0:T(8,128)S(1)}, f32[8,256,128]{2,1,0:T(8,128)S(1)}, u32[]{:S(2)}, u32[]{:S(2)}) collective-permute-start(f32[8,256,128]{2,1,0:T(8,128)S(1)} %project.2), channel_id=1, source_target_pairs={{0,1},{1,0},{2,3},{3,2},{4,5},{5,4},{6,7},{7,6},{8,9},{9,8},{10,11... | collective-permute-start | bytes 3145736 | tf_op jit(solution)/shard_map/ppermute | solution.py:454
  21.0 13.3 %collective-permute-start.5 = (f32[64,1024]{1,0:T(8,128)S(1)}, f32[64,1024]{1,0:T(8,128)S(1)}, u32[]{:S(2)}, u32[]{:S(2)}) collective-permute-start(f32[64,1024]{1,0:T(8,128)S(1)} %pad_maximum_fusion.g0), channel_id=1, source_target_pairs={{0,96},{1,25},{2,98},{3,27},{4,100},{5,29},{6,102},{7,31},{8,104},... | collective-permute-start | bytes 786440 | tf_op jit(solution)/shard_map/ppermute | solution.py:439
  23.8 10.5 %collective-permute-start.4 = (f32[64,1024]{1,0:T(8,128)S(1)}, f32[64,1024]{1,0:T(8,128)S(1)}, u32[]{:S(2)}, u32[]{:S(2)}) collective-permute-start(f32[64,1024]{1,0:T(8,128)S(1)} %pad_maximum_fusion.g0), channel_id=1, source_target_pairs={{0,64},{1,17},{2,66},{3,19},{4,68},{5,21},{6,70},{7,23},{8,72},{9,... | collective-permute-start | bytes 786440 | tf_op jit(solution)/shard_map/ppermute | solution.py:439
  24.6 9.9 %collective-permute-start.3 = (f32[64,1024]{1,0:T(8,128)S(1)}, f32[64,1024]{1,0:T(8,128)S(1)}, u32[]{:S(2)}, u32[]{:S(2)}) collective-permute-start(f32[64,1024]{1,0:T(8,128)S(1)} %pad_maximum_fusion.g0), channel_id=1, source_target_pairs={{0,32},{1,9},{2,34},{3,11},{4,36},{5,13},{6,38},{7,15},{8,40},{9,1... | collective-permute-start | bytes 786440 | tf_op jit(solution)/shard_map/ppermute | solution.py:439
  42.5 14.1 %collective-permute-start.9 = (f32[2,256,128]{2,1,0:T(8,128)S(1)}, f32[2,256,128]{2,1,0:T(8,128)S(1)}, u32[]{:S(2)}, u32[]{:S(2)}) collective-permute-start(f32[2,256,128]{2,1,0:T(8,128)S(1)} %get-tuple-element.105), channel_id=1, source_target_pairs={{0,6},{1,7},{2,0},{3,1},{4,2},{5,3},{6,4},{7,5},{8,14},{9,15},{10,... | collective-permute-start | bytes 786440 | tf_op jit(solution)/shard_map/ppermute | solution.py:458
  45.5 11.1 %collective-permute-start.8 = (f32[2,256,128]{2,1,0:T(8,128)S(1)}, f32[2,256,128]{2,1,0:T(8,128)S(1)}, u32[]{:S(2)}, u32[]{:S(2)}) collective-permute-start(f32[2,256,128]{2,1,0:T(8,128)S(1)} %get-tuple-element.106), channel_id=1, source_target_pairs={{0,4},{1,5},{2,6},{3,7},{4,0},{5,1},{6,2},{7,3},{8,12},{9,13},{10,... | collective-permute-start | bytes 786440 | tf_op jit(solution)/shard_map/ppermute | solution.py:458
  46.2 14.2 %collective-permute-start.7 = (f32[2,256,128]{2,1,0:T(8,128)S(1)}, f32[2,256,128]{2,1,0:T(8,128)S(1)}, u32[]{:S(2)}, u32[]{:S(2)}) collective-permute-start(f32[2,256,128]{2,1,0:T(8,128)S(1)} %get-tuple-element.107), channel_id=1, source_target_pairs={{0,2},{1,3},{2,4},{3,5},{4,6},{5,7},{6,0},{7,1},{8,10},{9,11},{10,... | collective-permute-start | bytes 786440 | tf_op jit(solution)/shard_map/ppermute | solution.py:458
  71.7 8.7 %collective-permute-start.15 = (f32[8,4096]{1,0:T(8,128)S(1)}, f32[8,4096]{1,0:T(8,128)S(1)}, u32[]{:S(2)}, u32[]{:S(2)}) collective-permute-start(f32[8,4096]{1,0:T(8,128)S(1)} %pad_maximum_fusion.1), channel_id=1, source_target_pairs={{0,24},{1,97},{2,26},{3,99},{4,28},{5,101},{6,30},{7,103},{8,0},{9... | collective-permute-start | bytes 393224 | tf_op jit(solution)/shard_map/ppermute | solution.py:468
  74.7 9.4 %collective-permute-start.13 = (f32[8,4096]{1,0:T(8,128)S(1)}, f32[8,4096]{1,0:T(8,128)S(1)}, u32[]{:S(2)}, u32[]{:S(2)}) collective-permute-start(f32[8,4096]{1,0:T(8,128)S(1)} %pad_maximum_fusion.1), channel_id=1, source_target_pairs={{0,8},{1,33},{2,10},{3,35},{4,12},{5,37},{6,14},{7,39},{8,16},{9,4... | collective-permute-start | bytes 393224 | tf_op jit(solution)/shard_map/ppermute | solution.py:468
  84.2 14.4 %collective-permute-start.18 = (f32[32,4096]{1,0:T(8,128)S(1)}, f32[32,4096]{1,0:T(8,128)S(1)}, u32[]{:S(2)}, u32[]{:S(2)}) collective-permute-start(f32[32,4096]{1,0:T(8,128)S(1)} %concatenate.24.n0), channel_id=1, source_target_pairs={{0,96},{1,25},{2,98},{3,27},{4,100},{5,29},{6,102},{7,31},{8,104},... | collective-permute-start | bytes 1572872 | tf_op jit(solution)/shard_map/ppermute | solution.py:439
  86.2 12.4 %collective-permute-start.17 = (f32[32,4096]{1,0:T(8,128)S(1)}, f32[32,4096]{1,0:T(8,128)S(1)}, u32[]{:S(2)}, u32[]{:S(2)}) collective-permute-start(f32[32,4096]{1,0:T(8,128)S(1)} %concatenate.24.n0), channel_id=1, source_target_pairs={{0,64},{1,17},{2,66},{3,19},{4,68},{5,21},{6,70},{7,23},{8,72},{9,... | collective-permute-start | bytes 1572872 | tf_op jit(solution)/shard_map/ppermute | solution.py:439
  87.7 14.8 %collective-permute-start.16 = (f32[32,4096]{1,0:T(8,128)S(1)}, f32[32,4096]{1,0:T(8,128)S(1)}, u32[]{:S(2)}, u32[]{:S(2)}) collective-permute-start(f32[32,4096]{1,0:T(8,128)S(1)} %concatenate.24.n0), channel_id=1, source_target_pairs={{0,32},{1,9},{2,34},{3,11},{4,36},{5,13},{6,38},{7,15},{8,40},{9,1... | collective-permute-start | bytes 1572872 | tf_op jit(solution)/shard_map/ppermute | solution.py:439
  88.1 14.4 %collective-permute-start.19 = (f32[32,4096]{1,0:T(8,128)S(1)}, f32[32,4096]{1,0:T(8,128)S(1)}, u32[]{:S(2)}, u32[]{:S(2)}) collective-permute-start(f32[32,4096]{1,0:T(8,128)S(1)} %concatenate.24.n0), channel_id=1, source_target_pairs={{0,1},{1,0},{2,3},{3,2},{4,5},{5,4},{6,7},{7,6},{8,9},{9,8},{10,11... | collective-permute-start | bytes 1572872 | tf_op jit(solution)/shard_map/ppermute | solution.py:470
  116.7 8.2 %collective-permute-start.25 = (f32[64,256]{1,0:T(8,128)S(1)}, f32[64,256]{1,0:T(8,128)S(1)}, u32[]{:S(2)}, u32[]{:S(2)}) collective-permute-start(f32[64,256]{1,0:T(8,128)S(1)} %get-tuple-element.70), channel_id=1, source_target_pairs={{0,24},{1,97},{2,26},{3,99},{4,28},{5,101},{6,30},{7,103},{8,0},{9... | collective-permute-start | bytes 196616 | tf_op jit(solution)/shard_map/ppermute | solution.py:434
  126.2 8.0 %collective-permute-start.27 = (f32[64,1024]{1,0:T(8,128)S(1)}, f32[64,1024]{1,0:T(8,128)S(1)}, u32[]{:S(2)}, u32[]{:S(2)}) collective-permute-start(f32[64,1024]{1,0:T(8,128)S(1)} %constant_dynamic-update-slice_fusion.g0), channel_id=1, source_target_pairs={{0,64},{1,17},{2,66},{3,19},{4,68},{5,21},{6,70},{7,23},{8,72},{9,... | collective-permute-start | bytes 786440 | tf_op jit(solution)/shard_map/ppermute | solution.py:439
  126.6 10.2 %collective-permute-start.26 = (f32[64,1024]{1,0:T(8,128)S(1)}, f32[64,1024]{1,0:T(8,128)S(1)}, u32[]{:S(2)}, u32[]{:S(2)}) collective-permute-start(f32[64,1024]{1,0:T(8,128)S(1)} %constant_dynamic-update-slice_fusion.g0), channel_id=1, source_target_pairs={{0,32},{1,9},{2,34},{3,11},{4,36},{5,13},{6,38},{7,15},{8,40},{9,1... | collective-permute-start | bytes 786440 | tf_op jit(solution)/shard_map/ppermute | solution.py:439
  139.3 7.4 %collective-permute-start.31 = (f32[64,256]{1,0:T(8,128)S(1)}, f32[64,256]{1,0:T(8,128)S(1)}, u32[]{:S(2)}, u32[]{:S(2)}) collective-permute-start(f32[64,256]{1,0:T(8,128)S(1)} %get-tuple-element.83), channel_id=1, source_target_pairs={{0,24},{1,97},{2,26},{3,99},{4,28},{5,101},{6,30},{7,103},{8,0},{9... | collective-permute-start | bytes 196616 | tf_op jit(solution)/shard_map/ppermute | solution.py:434
  147.4 8.0 %collective-permute-start.33 = (f32[64,1024]{1,0:T(8,128)S(1)}, f32[64,1024]{1,0:T(8,128)S(1)}, u32[]{:S(2)}, u32[]{:S(2)}) collective-permute-start(f32[64,1024]{1,0:T(8,128)S(1)} %constant_dynamic-update-slice_fusion.4.g0), channel_id=1, source_target_pairs={{0,64},{1,17},{2,66},{3,19},{4,68},{5,21},{6,70},{7,23},{8,72},{9,... | collective-permute-start | bytes 786440 | tf_op jit(solution)/shard_map/ppermute | solution.py:439
  148.3 9.8 %collective-permute-start.32 = (f32[64,1024]{1,0:T(8,128)S(1)}, f32[64,1024]{1,0:T(8,128)S(1)}, u32[]{:S(2)}, u32[]{:S(2)}) collective-permute-start(f32[64,1024]{1,0:T(8,128)S(1)} %constant_dynamic-update-slice_fusion.4.g0), channel_id=1, source_target_pairs={{0,32},{1,9},{2,34},{3,11},{4,36},{5,13},{6,38},{7,15},{8,40},{9,1... | collective-permute-start | bytes 786440 | tf_op jit(solution)/shard_map/ppermute | solution.py:439
  160.5 11.2 %collective-permute-start.37 = (f32[64,256]{1,0:T(8,128)S(1)}, f32[64,256]{1,0:T(8,128)S(1)}, u32[]{:S(2)}, u32[]{:S(2)}) collective-permute-start(f32[64,256]{1,0:T(8,128)S(1)} %get-tuple-element.89), channel_id=1, source_target_pairs={{0,24},{1,97},{2,26},{3,99},{4,28},{5,101},{6,30},{7,103},{8,0},{9... | collective-permute-start | bytes 196616 | tf_op jit(solution)/shard_map/ppermute | solution.py:434
  162.2 9.4 %collective-permute-start.36 = (f32[64,256]{1,0:T(8,128)S(1)}, f32[64,256]{1,0:T(8,128)S(1)}, u32[]{:S(2)}, u32[]{:S(2)}) collective-permute-start(f32[64,256]{1,0:T(8,128)S(1)} %get-tuple-element.89), channel_id=1, source_target_pairs={{0,16},{1,65},{2,18},{3,67},{4,20},{5,69},{6,22},{7,71},{8,24},{9,... | collective-permute-start | bytes 196616 | tf_op jit(solution)/shard_map/ppermute | solution.py:434
  163.3 8.3 %collective-permute-start.35 = (f32[64,256]{1,0:T(8,128)S(1)}, f32[64,256]{1,0:T(8,128)S(1)}, u32[]{:S(2)}, u32[]{:S(2)}) collective-permute-start(f32[64,256]{1,0:T(8,128)S(1)} %get-tuple-element.89), channel_id=1, source_target_pairs={{0,8},{1,33},{2,10},{3,35},{4,12},{5,37},{6,14},{7,39},{8,16},{9,4... | collective-permute-start | bytes 196616 | tf_op jit(solution)/shard_map/ppermute | solution.py:434
  172.9 8.0 %collective-permute-start.39 = (f32[64,1024]{1,0:T(8,128)S(1)}, f32[64,1024]{1,0:T(8,128)S(1)}, u32[]{:S(2)}, u32[]{:S(2)}) collective-permute-start(f32[64,1024]{1,0:T(8,128)S(1)} %constant_dynamic-update-slice_fusion.8.g0), channel_id=1, source_target_pairs={{0,64},{1,17},{2,66},{3,19},{4,68},{5,21},{6,70},{7,23},{8,72},{9,... | collective-permute-start | bytes 786440 | tf_op jit(solution)/shard_map/ppermute | solution.py:439
  173.3 11.7 %collective-permute-start.38 = (f32[64,1024]{1,0:T(8,128)S(1)}, f32[64,1024]{1,0:T(8,128)S(1)}, u32[]{:S(2)}, u32[]{:S(2)}) collective-permute-start(f32[64,1024]{1,0:T(8,128)S(1)} %constant_dynamic-update-slice_fusion.8.g0), channel_id=1, source_target_pairs={{0,32},{1,9},{2,34},{3,11},{4,36},{5,13},{6,38},{7,15},{8,40},{9,1... | collective-permute-start | bytes 786440 | tf_op jit(solution)/shard_map/ppermute | solution.py:439
  187.4 7.4 %collective-permute-start.43 = (f32[64,256]{1,0:T(8,128)S(1)}, f32[64,256]{1,0:T(8,128)S(1)}, u32[]{:S(2)}, u32[]{:S(2)}) collective-permute-start(f32[64,256]{1,0:T(8,128)S(1)} %get-tuple-element.95), channel_id=1, source_target_pairs={{0,24},{1,97},{2,26},{3,99},{4,28},{5,101},{6,30},{7,103},{8,0},{9... | collective-permute-start | bytes 196616 | tf_op jit(solution)/shard_map/ppermute | solution.py:434
  187.4 7.3 %collective-permute-start.42 = (f32[64,256]{1,0:T(8,128)S(1)}, f32[64,256]{1,0:T(8,128)S(1)}, u32[]{:S(2)}, u32[]{:S(2)}) collective-permute-start(f32[64,256]{1,0:T(8,128)S(1)} %get-tuple-element.95), channel_id=1, source_target_pairs={{0,16},{1,65},{2,18},{3,67},{4,20},{5,69},{6,22},{7,71},{8,24},{9,... | collective-permute-start | bytes 196616 | tf_op jit(solution)/shard_map/ppermute | solution.py:434
  196.1 8.0 %collective-permute-start.45 = (f32[64,1024]{1,0:T(8,128)S(1)}, f32[64,1024]{1,0:T(8,128)S(1)}, u32[]{:S(2)}, u32[]{:S(2)}) collective-permute-start(f32[64,1024]{1,0:T(8,128)S(1)} %constant_dynamic-update-slice_fusion.12.g0), channel_id=1, source_target_pairs={{0,64},{1,17},{2,66},{3,19},{4,68},{5,21},{6,70},{7,23},{8,72},{9,... | collective-permute-start | bytes 786440 | tf_op jit(solution)/shard_map/ppermute | solution.py:439
  196.4 10.7 %collective-permute-start.44 = (f32[64,1024]{1,0:T(8,128)S(1)}, f32[64,1024]{1,0:T(8,128)S(1)}, u32[]{:S(2)}, u32[]{:S(2)}) collective-permute-start(f32[64,1024]{1,0:T(8,128)S(1)} %constant_dynamic-update-slice_fusion.12.g0), channel_id=1, source_target_pairs={{0,32},{1,9},{2,34},{3,11},{4,36},{5,13},{6,38},{7,15},{8,40},{9,1... | collective-permute-start | bytes 786440 | tf_op jit(solution)/shard_map/ppermute | solution.py:439
  (34 other events, 214.8 us)
Sparse Core Ops, SparseCore 0:
  41.6 45.5 all-gather.2
